TPU v7x, 32 devices: a whole 2x2x4 slice. The times are simulated.
32 devices in a mesh: ctx: 4 (over z), seq: 8 (over y, x, core).
Axes of the slice: x: 2, y: 2, z: 4, core: 2. Of those that a mesh axis runs over, the one named last changes fastest.
Arguments:
- queries: bfloat16 [8192, 128], P(('seq', 'ctx')), may hold values from -6 to 6
- keys: bfloat16 [8192, 128], P(('seq', 'ctx')), may hold values from -6 to 6
- values: bfloat16 [8192, 1024], P(('seq', 'ctx')), may hold values from -6 to 6
- grad_output: bfloat16 [8192, 1024], P(('seq', 'ctx')), may hold values from -6 to 6
Outputs:
- attended: bfloat16 [8192, 1024], P(('seq', 'ctx'))
- grad_queries: bfloat16 [8192, 128], P(('seq', 'ctx'))
- grad_keys: bfloat16 [8192, 128], P(('seq', 'ctx'))
- grad_values: bfloat16 [8192, 1024], P(('seq', 'ctx'))
All inputs are finite; a program needn't handle non-finite values.
Results may differ from a plain program's by a relative error of at most 0.001.
Values sent between devices are 32-bit elements; how exact they have to be, the bound alone decides.
A program may use at most 128 MiB of HBM per device.

v0:
```python
import math

import jax
import jax.numpy as jnp
import numpy as np
from jax import lax
from jax.sharding import PartitionSpec as P

HEADS = 8
QK_DIM = 16
HEAD_DIM = 128


HIGHEST = lax.Precision.HIGHEST


def carried_in(part, axis, combine, identity, reverse):
    count = lax.axis_size(axis)
    place = lax.axis_index(axis)
    ahead = count - 1 - place if reverse else place
    gathered = jax.tree.map(lambda a: lax.all_gather(a, axis), part)
    state = jax.tree.map(lambda a, e: jnp.zeros_like(a) + jnp.asarray(e, a.dtype), part, identity)

    def one(turn, state):
        source = count - 1 - turn if reverse else turn
        return combine(
            state, jax.tree.map(lambda a: lax.dynamic_index_in_dim(a, source, 0, False), gathered)
        )

    return lax.fori_loop(0, ahead, one, state)


def features(entries):
    width = entries.shape[1]
    upper, lower = np.triu_indices(width)
    factors = np.where(upper == lower, 1.0, math.sqrt(2.0)) / math.sqrt(2.0 * width)
    ones = jnp.ones_like(entries[:, :1, :])
    linear = entries / math.sqrt(math.sqrt(width))
    square = (
        entries[:, upper, :]
        * entries[:, lower, :]
        * jnp.asarray(factors, entries.dtype)[None, :, None]
    )
    return jnp.concatenate([ones, linear, square], axis=1)


def add_pairs(earlier, later):
    return (earlier[0] + later[0], earlier[1] + later[1])


def combine(pair, reverse):
    zeros = (jnp.zeros_like(pair[0]), jnp.zeros_like(pair[1]))
    inner = carried_in(pair, "ctx", add_pairs, zeros, reverse)
    total = lax.psum((pair[0], pair[1]), "ctx")
    outer = carried_in(total, "seq", add_pairs, zeros, reverse)
    return add_pairs(outer, inner)


def per_device(queries, keys, values, grad_output):
    length = queries.shape[0]
    query_half = queries.reshape(length, HEADS, QK_DIM)
    key_half = keys.reshape(length, HEADS, QK_DIM)
    query = query_half.astype(jnp.float32)
    key_rows = key_half.astype(jnp.float32)
    value = values.astype(jnp.float32).reshape(length, HEADS, HEAD_DIM)
    grad = grad_output.astype(jnp.float32).reshape(length, HEADS, HEAD_DIM)
    left, left_pull = jax.vjp(features, jnp.transpose(query, (1, 2, 0)))
    right, right_pull = jax.vjp(features, jnp.transpose(key_rows, (1, 2, 0)))
    state = jnp.einsum("hfs,she->hfe", right, value, precision=HIGHEST)
    norm = jnp.sum(right, axis=-1)
    prior_state, prior_norm = combine((state, norm), False)
    dots = jnp.einsum(
        "thd,shd->hts", query_half, key_half, preferred_element_type=jnp.float32
    ) / math.sqrt(QK_DIM)
    causal = jnp.arange(length)[:, None] >= jnp.arange(length)[None, :]
    kernel = jnp.where(causal[None], 1.0 + dots + 0.5 * dots * dots, 0.0)
    numer = jnp.einsum("hts,she->the", kernel, value, precision=HIGHEST)
    numer = numer + jnp.einsum("hft,hfe->the", left, prior_state, precision=HIGHEST)
    denom = jnp.sum(kernel, axis=-1).T + jnp.einsum(
        "hft,hf->th", left, prior_norm, precision=HIGHEST
    )
    output = numer / denom[:, :, None]
    scaled = grad / denom[:, :, None]
    share = jnp.sum(grad * output, axis=-1) / denom
    term_state = jnp.einsum("hft,the->hfe", left, scaled, precision=HIGHEST)
    term_norm = jnp.einsum("hft,th->hf", left, share, precision=HIGHEST)
    later_state, later_norm = combine((term_state, term_norm), True)
    direct = jnp.einsum("the,she->hts", scaled, value, precision=HIGHEST) - share.T[:, :, None]
    grad_kernel = jnp.where(causal[None], direct, 0.0)
    grad_left = (
        jnp.einsum("hfe,the->hft", prior_state, scaled, precision=HIGHEST)
        - prior_norm[:, :, None] * share.T[:, None, :]
    )
    grad_right = (
        jnp.einsum("hfe,she->hfs", later_state, value, precision=HIGHEST) - later_norm[:, :, None]
    )
    grad_value = jnp.einsum("hts,the->she", kernel, scaled, precision=HIGHEST)
    grad_value = grad_value + jnp.einsum("hfs,hfe->she", right, later_state, precision=HIGHEST)
    grad_dots = grad_kernel * (1.0 + dots) / math.sqrt(QK_DIM)
    grad_query = jnp.einsum("hts,shd->thd", grad_dots, key_rows, precision=HIGHEST)
    grad_query = grad_query + jnp.transpose(left_pull(grad_left)[0], (2, 0, 1))
    grad_key = jnp.einsum("hts,thd->shd", grad_dots, query, precision=HIGHEST)
    grad_key = grad_key + jnp.transpose(right_pull(grad_right)[0], (2, 0, 1))
    return (
        output.reshape(length, HEADS * HEAD_DIM).astype(jnp.bfloat16),
        grad_query.reshape(length, HEADS * QK_DIM).astype(jnp.bfloat16),
        grad_key.reshape(length, HEADS * QK_DIM).astype(jnp.bfloat16),
        grad_value.reshape(length, HEADS * HEAD_DIM).astype(jnp.bfloat16),
    )


def solution(mesh):
    placed = (
        P(("seq", "ctx"), None),
        P(("seq", "ctx"), None),
        P(("seq", "ctx"), None),
        P(("seq", "ctx"), None),
    )
    return jax.shard_map(
        per_device,
        mesh=mesh,
        in_specs=placed,
        out_specs=(
            P(("seq", "ctx"), None),
            P(("seq", "ctx"), None),
            P(("seq", "ctx"), None),
            P(("seq", "ctx"), None),
        ),
        check_vma=False,
    )
```

profile of v0, /device:TPU:0, one launch (start us, length us, event | category | flops | bytes accessed | tf_op | source)
XLA Modules:
  0.0 402.0 jit_solution(2930540588218161256)
XLA Ops:
  10.5 1.8 gather_fusion.1
  12.5 1.8 gather_fusion.2
  14.3 1.8 gather_fusion.3
  16.2 4.2 %fusion.12 = (f32[8,136,256]{2,1,0:T(8,128)}, f32[8,136,256]{2,1,0:T(8,128)S(1)}) fusion(f32[136,8,256]{2,1,0:T(8,128)} %gather_fusion.3, f32[136,8,256]{2,1,0:T(8,128)} %gather_fusion.2, f32[136]{0:T(256)S(1)} %copy-done.29, f32[136,8,256]{2,1,0:T(8,128)} %gather_fusion.1, f32[136,8,256]{2,1,0:T(8,128)S(1)} %gather_fusion), kind=kLoop, calls=%fused_computation.47 | loop fusion | flops 1114112 | bytes 6685216 | tf_op jit(solution)/shard_map/jvp()/mul | solution.py:40
  21.3 1.2 copy.91
  24.0 44.9 %all-reduce.3.cloned.1.call-done = f32[1,8,153,128]{3,2,1,0:T(8,128)} async-done(((f32[1,8,153,128]{3,2,1,0:T(8,128)}), f32[1,8,153,128]{3,2,1,0:T(8,128)}) %all-reduce.3.cloned.1.call-update) | async-done | bytes 626704 | tf_op jit(solution)/shard_map/psum | solution.py:54
  68.9 2.3 copy.89
  71.2 1.2 copy.97
  72.9 10.6 %psum.29 = f32[1,8,153]{2,1,0:T(8,128)S(1)} all-reduce(f32[1,8,153]{2,1,0:T(8,128)S(1)} %bitcast.194), channel_id=1, replica_groups=mesh['ctx'=4,'seq'=8] {'ctx'}, use_global_device_ids=true, to_apply=%region_2.3 | all-reduce | flops 1224 | bytes 9792 | tf_op jit(solution)/shard_map/psum | solution.py:54
  83.6 18.5 %all-gather.1 = f32[32,153]{1,0:T(8,128)S(1)} all-gather(f32[8,153]{1,0:T(8,128)S(1)} %fusion.17), channel_id=3, replica_groups=mesh['ctx'=4,'seq'=8] {'ctx'}, dimensions={0}, use_global_device_ids=true | all-gather | bytes 24480 | tf_op jit(solution)/shard_map/all_gather | solution.py:21
  102.1 9.4 %all_gather.51 = f32[8,8,153]{2,1,0:T(8,128)S(1)} all-gather(f32[1,8,153]{2,1,0:T(8,128)S(1)} %psum.29), channel_id=1, replica_groups=mesh['ctx'=4,'seq'=8] {'seq'}, dimensions={0}, use_global_device_ids=true | all-gather | bytes 44064 | tf_op jit(solution)/shard_map/all_gather | solution.py:21
  111.6 2.1 fusion.22
  113.7 9.8 %all-gather.13.cloned.1.call-done = f32[32,153,128]{2,0,1:T(8,128)} async-done(((f32[8,153,128]{2,0,1:T(8,128)}), f32[32,153,128]{2,0,1:T(8,128)}) %all-gather.13.cloned.1.call-update) | async-done | bytes 2506768 | tf_op jit(solution)/shard_map/all_gather | solution.py:21
  123.6 40.2 %all-gather.9.cloned.1.call-done = f32[8,8,153,128]{3,1,2,0:T(8,128)} async-done(((f32[1,8,153,128]{3,1,2,0:T(8,128)}), f32[8,8,153,128]{3,1,2,0:T(8,128)}) %all-gather.9.cloned.1.call-update) | async-done | bytes 5013520 | tf_op jit(solution)/shard_map/all_gather | solution.py:21
  163.9 2.2 fusion.41
  166.2 2.7 fusion.54
  169.8 1.2 copy.111
  172.4 51.6 %all-reduce.5.cloned.1.call-done = f32[1,8,153,128]{3,2,1,0:T(8,128)} async-done(((f32[1,8,153,128]{3,2,1,0:T(8,128)}), f32[1,8,153,128]{3,2,1,0:T(8,128)}) %all-reduce.5.cloned.1.call-update) | async-done | bytes 626704 | tf_op jit(solution)/shard_map/psum | solution.py:54
  224.1 2.3 copy.109
  226.4 3.2 convolution_bitcast_fusion
  229.6 2.1 multiply_reduce_fusion
  232.3 1.4 fusion.39
  234.7 10.9 %psum.31 = f32[1,8,153]{2,1,0:T(8,128)S(1)} all-reduce(f32[1,8,153]{2,1,0:T(8,128)S(1)} %bitcast.195), channel_id=1, replica_groups=mesh['ctx'=4,'seq'=8] {'ctx'}, use_global_device_ids=true, to_apply=%region_12.13 | all-reduce | flops 1224 | bytes 9792 | tf_op jit(solution)/shard_map/psum | solution.py:54
  245.6 16.6 %all-gather.3 = f32[32,153]{1,0:T(8,128)S(1)} all-gather(f32[8,153]{1,0:T(8,128)S(1)} %bitcast.196), channel_id=5, replica_groups=mesh['ctx'=4,'seq'=8] {'ctx'}, dimensions={0}, use_global_device_ids=true | all-gather | bytes 24480 | tf_op jit(solution)/shard_map/all_gather | solution.py:21
  262.2 12.5 %all_gather.59 = f32[8,8,153]{2,1,0:T(8,128)S(1)} all-gather(f32[1,8,153]{2,1,0:T(8,128)S(1)} %psum.31), channel_id=1, replica_groups=mesh['ctx'=4,'seq'=8] {'seq'}, dimensions={0}, use_global_device_ids=true | all-gather | bytes 44064 | tf_op jit(solution)/shard_map/all_gather | solution.py:21
  275.4 3.7 convolution_subtract_fusion
  279.2 3.6 fusion.21
  282.8 2.9 multiply_multiply_fusion
  285.8 4.3 %while.55 = (s32[]{:T(128)}, f32[8,153,128]{2,1,0:T(8,128)S(1)}, f32[8,153]{1,0:T(8,128)S(1)}, s32[]{:T(128)}, f32[4,8,153,128]{3,1,0,2:T(8,128)}, /*index=5*/f3...) while((s32[]{:T(128)}, f32[8,153,128]{2,1,0:T(8,128)S(1)}, f32[8,153]{1,0:T(8,128)S(1)}, ...), condition=%wide.region_16.17_spmd, body=%wide.region_15.16_spmd.sunk | while | flops 157902 | bytes 3148283 | solution.py:30
  285.8 1.2 constant_dynamic-slice_fusion.11
  287.2 1.2 constant_dynamic-slice_fusion.11
  288.7 1.1 constant_dynamic-slice_fusion.11
  290.1 29.1 %all-gather.11.cloned.1.call-done = f32[8,8,153,128]{3,1,2,0:T(8,128)} async-done(((f32[1,8,153,128]{3,1,2,0:T(8,128)}), f32[8,8,153,128]{3,1,2,0:T(8,128)}) %all-gather.11.cloned.1.call-update) | async-done | bytes 5013520 | tf_op jit(solution)/shard_map/all_gather | solution.py:21
  319.2 9.9 %while.54 = (s32[]{:T(128)}, f32[8,153,128]{2,1,0:T(8,128)S(1)}, f32[8,153]{1,0:T(8,128)S(1)}, s32[]{:T(128)}, f32[8,8,153,128]{3,1,2,0:T(8,128)}, /*index=5*/f3...) while((s32[]{:T(128)}, f32[8,153,128]{2,1,0:T(8,128)S(1)}, f32[8,153]{1,0:T(8,128)S(1)}, ...), condition=%wide.region_14.15_spmd, body=%wide.region_13.14_spmd.sunk | while | flops 157902 | bytes 3148283 | solution.py:30
  319.4 1.1 constant_dynamic-slice_fusion.10
  320.8 1.1 constant_dynamic-slice_fusion.10
  329.2 3.3 fusion.6
  335.1 5.1 %fusion.16 = (f32[136,8,256]{2,0,1:T(8,128)S(1)}, f32[136,8,256]{2,0,1:T(8,128)S(1)}, f32[136,8,256]{2,0,1:T(8,128)S(1)}, f32[136,8,256]{2,0,1:T(8,128)}) fusion(f32[136,8,256]{2,1,0:T(8,128)S(1)} %copy-done.2, f32[8,153,256]{2,1,0:T(8,128)S(1)} %convolution_subtract_fusion.1, f32[136]{0:T(256)S(1)} %copy-done.30, f32[136,8,256]{2,1,0:T(8,128)S(1)} %copy-done.3, ...), kind=kLoop, calls=%fused_computation.55 | loop fusion | flops 1671168 | bytes 11141664 | tf_op jit(solution)/shard_map/transpose(jvp())/mul | solution.py:40
  340.2 1.3 copy.114
  341.5 1.3 copy.115
  342.9 11.8 %scatter_fusion.2 = f32[8,16,256]{2,0,1:T(8,128)S(1)} fusion(f32[8,16,256]{2,0,1:T(8,128)S(1)} %broadcast.52.clone.3, s32[136]{0:T(256)S(1)} %copy-done.27, f32[136,8,256]{2,1,0:T(8,128)} %copy.114), kind=kCustom, calls=%fused_computation.6 | custom fusion | flops 278528 | bytes 3342880 | tf_op jit(solution)/shard_map/transpose(jvp())/scatter-add | solution.py:41
  354.7 12.0 %scatter_fusion.3 = f32[8,16,256]{2,0,1:T(8,128)S(1)} fusion(f32[8,16,256]{2,0,1:T(8,128)S(1)} %broadcast.52.clone.2, s32[136]{0:T(256)S(1)} %copy-done.26, f32[136,8,256]{2,1,0:T(8,128)} %copy.115), kind=kCustom, calls=%fused_computation.7 | custom fusion | flops 278528 | bytes 3342880 | tf_op jit(solution)/shard_map/transpose(jvp())/scatter-add | solution.py:40
  366.7 2.6 fusion.9
  370.1 2.6 copy.103
  372.7 1.3 copy.104
  374.1 11.8 %scatter_fusion = f32[8,16,256]{2,0,1:T(8,128)S(1)} fusion(f32[8,16,256]{2,0,1:T(8,128)S(1)} %broadcast.52.clone.1, s32[136]{0:T(256)S(1)} %copy-done.27, f32[136,8,256]{2,1,0:T(8,128)} %copy.103), kind=kCustom, calls=%fused_computation.4 | custom fusion | flops 278528 | bytes 3342880 | tf_op jit(solution)/shard_map/transpose(jvp())/scatter-add | solution.py:41
  385.9 6.1 %scatter_fusion.1 = f32[8,16,256]{2,0,1:T(8,128)S(1)} fusion(f32[8,16,256]{2,0,1:T(8,128)S(1)} %broadcast.52.clone, s32[136]{0:T(256)S(1)} %copy-done.26, f32[136,8,256]{2,1,0:T(8,128)S(1)} %copy-done.6), kind=kCustom, calls=%fused_computation.5 | custom fusion | flops 278528 | bytes 3342880 | tf_op jit(solution)/shard_map/transpose(jvp())/scatter-add | solution.py:40
  392.0 2.4 fusion.10
  (142 shorter events, 23.2 us)
Async XLA Ops:
  7.2 13.2 %copy-start = (bf16[256,1024]{1,0:T(8,128)(2,1)S(1)}, bf16[256,1024]{1,0:T(8,128)(2,1)}, u32[]{:S(2)}) copy-start(bf16[256,1024]{1,0:T(8,128)(2,1)} %param.24) | copy-start | bytes 1572868
  10.4 5.7 %copy-start.1 = (f32[136,8,256]{2,1,0:T(8,128)}, f32[136,8,256]{2,1,0:T(8,128)S(1)}, u32[]{:S(2)}) copy-start(f32[136,8,256]{2,1,0:T(8,128)S(1)} %gather_fusion) | copy-start | bytes 3342340
  10.5 1.8 copy-start.18
  12.4 99.2 %copy-start.11 = (bf16[256,128]{0,1:T(8,128)(2,1)}, bf16[256,128]{0,1:T(8,128)(2,1)S(1)}, u32[]{:S(2)}) copy-start(bf16[256,128]{0,1:T(8,128)(2,1)S(1)} %copy.80) | copy-start | bytes 196612
  14.3 1.8 copy-start.29
  16.1 56.3 %copy-start.8 = (f32[8,16,256]{2,1,0:T(8,128)}, f32[8,16,256]{2,1,0:T(8,128)S(1)}, u32[]{:S(2)}) copy-start(f32[8,16,256]{2,1,0:T(8,128)S(1)} %broadcast_multiply_fusion.1) | copy-start | bytes 393220
  16.2 147.7 %copy-start.24 = (f32[153]{0:T(256)}, f32[153]{0:T(256)S(1)}, u32[]{:S(2)}) copy-start(f32[153]{0:T(256)S(1)} %pad.3.clone) | copy-start | bytes 1840
  21.2 1.2 copy-start.4
  22.5 46.4 %all-reduce.3.cloned.1.call-start = ((), (), s32[]{:S(2)}) async-start(), calls=%async_computation | async-start | bytes 1310720 | tf_op jit(solution)/shard_map/psum | solution.py:54
  23.2 48.0 %copy-start.15 = (bf16[256,1024]{1,0:T(8,128)(2,1)S(1)}, bf16[256,1024]{1,0:T(8,128)(2,1)}, u32[]{:S(2)}) copy-start(bf16[256,1024]{1,0:T(8,128)(2,1)} %param.25) | copy-start | bytes 1572868
  23.2 100.3 %all-gather.13.cloned.1.call-start = ((), (), s32[]{:S(2)}) async-start(), calls=%async_computation.4 | async-start | bytes 3133440 | tf_op jit(solution)/shard_map/all_gather | solution.py:21
  23.9 139.8 %all-gather.9.cloned.1.call-start = ((), (), s32[]{:S(2)}) async-start(), calls=%async_computation.1 | async-start | bytes 5640192 | tf_op jit(solution)/shard_map/all_gather | solution.py:21
  111.5 114.9 %copy-start.19 = (pred[256,256]{0,1:T(8,128)(4,1)}, pred[256,256]{0,1:T(8,128)(4,1)S(1)}, u32[]{:S(2)}) copy-start(pred[256,256]{0,1:T(8,128)(4,1)S(1)} %iota_compare_fusion) | copy-start | bytes 196612
  111.5 54.6 %copy-start.16 = (f32[8,16,256]{2,1,0:T(8,128)}, f32[8,16,256]{2,1,0:T(8,128)S(1)}, u32[]{:S(2)}) copy-start(f32[8,16,256]{2,1,0:T(8,128)S(1)} %broadcast_multiply_fusion) | copy-start | bytes 393220
  113.7 52.5 %copy-start.21 = (f32[8,256]{1,0:T(8,128)}, f32[8,256]{1,0:T(8,128)S(1)}, u32[]{:S(2)}) copy-start(f32[8,256]{1,0:T(8,128)S(1)} %get-tuple-element.338) | copy-start | bytes 24580
  163.9 2.3 copy-start.9
  163.9 5.1 %copy-start.28 = (f32[8,153]{1,0:T(8,128)}, f32[8,153]{1,0:T(8,128)S(1)}, u32[]{:S(2)}) copy-start(f32[8,153]{1,0:T(8,128)S(1)} %add.159) | copy-start | bytes 14692
  166.2 2.8 copy-start.22
  169.0 0.9 copy-start.7
  171.0 53.0 %all-reduce.5.cloned.1.call-start = ((), (), s32[]{:S(2)}) async-start(), calls=%async_computation.2 | async-start | bytes 1310720 | tf_op jit(solution)/shard_map/psum | solution.py:54
  171.6 114.1 %all-gather.15.cloned.1.call-start = ((), (), s32[]{:S(2)}) async-start(), calls=%async_computation.5 | async-start | bytes 3133440 | tf_op jit(solution)/shard_map/all_gather | solution.py:21
  172.2 147.0 %all-gather.11.cloned.1.call-start = ((), (), s32[]{:S(2)}) async-start(), calls=%async_computation.3 | async-start | bytes 5640192 | tf_op jit(solution)/shard_map/all_gather | solution.py:21
  226.4 3.2 copy-start.10
  226.4 3.2 copy-start.13
  226.4 3.2 copy-start.17
  226.4 3.2 copy-start.25
  231.7 0.6 copy-start.23
  275.4 3.8 copy-start.14
  275.4 3.8 copy-start.20
  275.4 3.7 copy-start.31
  333.5 1.2 copy-start.2
  333.5 1.6 copy-start.3
  333.5 1.6 copy-start.30
  335.1 5.1 %copy-start.5 = (f32[8,153,256]{2,1,0:T(8,128)}, f32[8,153,256]{2,1,0:T(8,128)S(1)}, u32[]{:S(2)}) copy-start(f32[8,153,256]{2,1,0:T(8,128)S(1)} %convolution_subtract_fusion.1) | copy-start | bytes 3760132
  341.5 1.3 copy-start.27
  342.9 11.8 %copy-start.26 = (s32[136]{0:T(256)S(1)}, s32[136]{0:T(256)}, u32[]{:S(2)}) copy-start(s32[136]{0:T(256)} %constant.131) | copy-start | bytes 1636
  354.7 12.0 %copy-start.12 = (bf16[256,128]{0,1:T(8,128)(2,1)S(1)}, bf16[256,128]{0,1:T(8,128)(2,1)}, u32[]{:S(2)}) copy-start(bf16[256,128]{0,1:T(8,128)(2,1)} %copy-done.11) | copy-start | bytes 196612
  374.1 11.8 %copy-start.6 = (f32[136,8,256]{2,1,0:T(8,128)S(1)}, f32[136,8,256]{2,1,0:T(8,128)}, u32[]{:S(2)}) copy-start(f32[136,8,256]{2,1,0:T(8,128)} %copy.104) | copy-start | bytes 3342340
Sparse Core Ops, SparseCore 0:
  25.6 43.1 all-reduce.2
  70.4 53.0 all-gather.12
  125.4 38.3 all-gather.8
  173.9 50.1 all-reduce.4
  225.5 53.4 all-gather.14
  280.7 38.3 all-gather.10
where the time goes:
time: 404 us; the launch traced here: 402 us
  waiting for transfers between devices  178 us (44%)
  blocking collectives  78.5 us (19%)
  other arithmetic  55.9 us (14%)
  local copies, waits for them, and re-layouts  39.8 us (10%)
  matrix products  33.9 us (8%)
  between operations  14.7 us (4%)
    psum x2, waiting for transfers between devices, combine(): total = lax.psum((pair[0], pair[1]), 'ctx')  96.5 us
    all_gather x4, waiting for transfers between devices, carried_in(): gathered = jax.tree.map(lambda a: lax.all_gather(a, axis), part)  79.1 us
    all_gather x4, blocking collectives, carried_in(): gathered = jax.tree.map(lambda a: lax.all_gather(a, axis), part)  57 us
    scatter-add x2, other arithmetic, features(): entries[:, lower, :]  23.5 us
    psum x2, blocking collectives, combine(): total = lax.psum((pair[0], pair[1]), 'ctx')  21.5 us
    scatter-add x2, other arithmetic, features(): entries[:, upper, :] * entries[:, lower, :]  18.2 us
    dynamic_slice x10, local copies, waits for them, and re-layouts, one(): lax.dynamic_index_in_dim(a, source, 0, False)  11.4 us
    mul x2, other arithmetic, features(): entries[:, upper, :] * entries[:, lower, :]  9.27 us
  transfers between devices with their start and end apart: 6, of which 5 were waited for; matrix products, arithmetic and copies ran while one was open for 8% of the time, Pallas kernels for 0%

commit v1 on v0

v1 whole, which is shorter than its diff:
```python
import functools
import math

import jax
import jax.numpy as jnp
import numpy as np
from jax import lax
from jax.experimental import pallas as pl
from jax.experimental.pallas import tpu as pltpu
from jax.sharding import PartitionSpec as P

HEADS = 8
QK_DIM = 16
HEAD_DIM = 128
FEATURES = 153
ROWS = 160
LANES = 128
MESH = pl.DeviceIdType.MESH
NN = (((1,), (0,)), ((), ()))
NT = (((1,), (1,)), ((), ()))
TN = (((0,), (0,)), ((), ()))


def tables():
    upper, lower = np.triu_indices(QK_DIM)
    pick_a = np.zeros((HEADS, ROWS, LANES), np.float32)
    pick_b = np.zeros((HEADS, ROWS, LANES), np.float32)
    aux = np.zeros((8, ROWS), np.float32)
    aux[0, 0] = 1.0
    aux[1, : 1 + QK_DIM] = 1.0
    aux[2, 0] = 1.0
    aux[2, 1 : 1 + QK_DIM] = 1.0 / math.sqrt(math.sqrt(QK_DIM))
    aux[2, 1 + QK_DIM : FEATURES] = np.where(upper == lower, 1.0, math.sqrt(2.0)) / math.sqrt(
        2.0 * QK_DIM
    )
    for head in range(HEADS):
        base = head * QK_DIM
        for i in range(QK_DIM):
            pick_a[head, 1 + i, base + i] = 1.0
        for n, (i, j) in enumerate(zip(upper, lower)):
            pick_a[head, 1 + QK_DIM + n, base + i] = 1.0
            pick_b[head, 1 + QK_DIM + n, base + j] = 1.0
    aux_column = np.zeros((ROWS, LANES), np.float32)
    aux_column[:, :8] = aux.T
    return (
        jnp.asarray(pick_a, jnp.bfloat16),
        jnp.asarray(pick_b, jnp.bfloat16),
        jnp.asarray(aux),
        jnp.asarray(aux_column),
    )


def dot(a, b, dims=NN):
    return lax.dot_general(a, b, dims, preferred_element_type=jnp.float32)


def split(x):
    high = x.astype(jnp.bfloat16)
    return high, (x - high.astype(jnp.float32)).astype(jnp.bfloat16)


def dot2(pair, b, dims=NN):
    return dot(pair[0], b, dims) + dot(pair[1], b, dims)


def dot2r(a, pair, dims=NN):
    return dot(a, pair[0], dims) + dot(a, pair[1], dims)


def dot3(x, y, dims=NN):
    return dot(x[0], y[0], dims) + (dot(x[0], y[1], dims) + dot(x[1], y[0], dims))


def features_by_row(pick_a, pick_b, aux_column, x):
    a = dot(pick_a, x, NT) + aux_column[:, 0:1]
    b = dot(pick_b, x, NT) + aux_column[:, 1:2]
    return a * b * aux_column[:, 2:3]


def factors_by_token(pick_a, pick_b, aux, x):
    a = dot(x, pick_a, NT) + aux[0:1, :]
    b = dot(x, pick_b, NT) + aux[1:2, :]
    return a, b


def put_state(ref, state, norm):
    ref[0] = state
    ref[0, FEATURES : FEATURES + 1, :] = norm[0:1, :LANES]
    ref[0, FEATURES + 1 : FEATURES + 2, : ROWS - LANES] = norm[0:1, LANES:ROWS]


def norm_of(ref):
    return jnp.concatenate(
        [
            ref[0, FEATURES : FEATURES + 1, :],
            ref[0, FEATURES + 1 : FEATURES + 2, : ROWS - LANES],
        ],
        axis=1,
    )


def key_state_kernel(k_ref, v_ref, a_ref, b_ref, auxc_ref, x_ref):
    phi = split(features_by_row(a_ref[0], b_ref[0], auxc_ref, k_ref[...]))
    ones = jnp.ones((8, k_ref.shape[0]), jnp.bfloat16)
    put_state(x_ref, dot2(phi, v_ref[...]), dot2r(ones, phi, NT))


def pull(grad, a, b, pick_a, pick_b):
    return dot2(split(grad * b), pick_a) + dot2(split(grad * a), pick_b)


def middle_kernel(
    q_ref, k_ref, v_ref, g_ref, p_ref, a_ref, b_ref, aux_ref, auxc_ref,
    out_ref, gq_ref, x_ref, gk_ref, gv_ref, gq_acc, gk_acc,
):
    head = pl.program_id(0)
    length = q_ref.shape[0]
    q, k, v, g = q_ref[...], k_ref[...], v_ref[...], g_ref[...]
    pick_a, pick_b = a_ref[0], b_ref[0]
    scale = 1.0 / math.sqrt(QK_DIM)
    mine = lax.broadcasted_iota(jnp.int32, (length, LANES), 1) // QK_DIM == head
    q_mine = jnp.where(mine, q, jnp.zeros_like(q))
    k_mine = jnp.where(mine, k, jnp.zeros_like(k))
    s = dot(q_mine, k, NT) * scale
    causal = lax.broadcasted_iota(jnp.int32, (length, length), 0) >= lax.broadcasted_iota(
        jnp.int32, (length, length), 1
    )
    kern = split(jnp.where(causal, 1.0 + s + 0.5 * s * s, 0.0))
    local = dot2(kern, jnp.concatenate([v, jnp.ones_like(v)], axis=1))
    a, b = factors_by_token(pick_a, pick_b, aux_ref, q)
    phi = a * b * aux_ref[2:3, :]
    prior = split(p_ref[0])
    prior_norm = norm_of(p_ref)
    den = local[:, HEAD_DIM:] + jnp.sum(phi * prior_norm, axis=1, keepdims=True)
    rden = 1.0 / den
    out = (local[:, :HEAD_DIM] + dot3(split(phi), prior)) * rden
    out_ref[...] = out.astype(jnp.bfloat16)
    g32 = g.astype(jnp.float32)
    scaled = split(g32 * rden)
    weighed = g32 * out * rden
    share = jnp.sum(weighed, axis=1, keepdims=True)
    share_row = split(dot2r(jnp.ones((8, LANES), jnp.bfloat16), split(weighed), NT))
    phi_row = split(features_by_row(pick_a, pick_b, auxc_ref, q))
    put_state(x_ref, dot3(phi_row, scaled), dot3(share_row, phi_row, NT))
    rden_column = rden[:, 0:1]
    direct = dot(g, v, NT) * rden_column - share
    grad_dots = split(jnp.where(causal, direct * (1.0 + s) * scale, 0.0))
    gv_ref[...] = dot3(kern, scaled, TN)
    grad_phi = dot2r(g, prior, NT) * rden_column - share * prior_norm
    grad_q = dot2(grad_dots, k_mine) + pull(grad_phi * aux_ref[2:3, :], a, b, pick_a, pick_b)
    grad_k = dot2(grad_dots, q_mine, TN)

    @pl.when(head == 0)
    def _():
        gq_acc[...] = grad_q
        gk_acc[...] = grad_k

    @pl.when(head > 0)
    def _():
        gq_acc[...] += grad_q
        gk_acc[...] += grad_k

    @pl.when(head == HEADS - 1)
    def _():
        gq_ref[...] = gq_acc[...].astype(jnp.bfloat16)
        gk_ref[...] = gk_acc[...]


def last_kernel(
    k_ref, v_ref, l_ref, gk_in, gv_in, a_ref, b_ref, aux_ref, gk_ref, gv_ref, gk_acc
):
    head = pl.program_id(0)
    k, v = k_ref[...], v_ref[...]
    pick_a, pick_b = a_ref[0], b_ref[0]
    later = split(l_ref[0])
    later_norm = norm_of(l_ref)
    a, b = factors_by_token(pick_a, pick_b, aux_ref, k)
    factor = aux_ref[2:3, :]
    gv_ref[...] = (gv_in[...] + dot3(split(a * b * factor), later)).astype(jnp.bfloat16)
    grad_phi = dot2r(v, later, NT) - later_norm
    grad_k = pull(grad_phi * factor, a, b, pick_a, pick_b)

    @pl.when(head == 0)
    def _():
        gk_acc[...] = gk_in[...] + grad_k

    @pl.when(head > 0)
    def _():
        gk_acc[...] += grad_k

    @pl.when(head == HEADS - 1)
    def _():
        gk_ref[...] = gk_acc[...].astype(jnp.bfloat16)


def scan_kernel(
    n_ctx, n_seq, reverse, x_ref, p_ref, got, tot, before, up, down,
    send_sem, recv_sem,
):
    rounds = n_seq.bit_length() - 1
    chunks = x_ref.shape[0]
    up_at, down_at = rounds, rounds + 1
    ctx, seq = lax.axis_index("ctx"), lax.axis_index("seq")
    if reverse:
        place, line = n_ctx - 1 - ctx, n_seq - 1 - seq
        step = -1
    else:
        place, line = ctx, seq
        step = 1
    high = [(line // (1 << r)) % 2 for r in range(rounds)]
    partner = [seq + step * (1 << r) * (1 - 2 * high[r]) for r in range(rounds)]
    has_above = place < n_ctx - 1
    has_below = place > 0
    above = lax.rem(ctx + step + n_ctx, n_ctx)
    below = lax.rem(ctx - step + n_ctx, n_ctx)

    barrier = pltpu.get_barrier_semaphore()
    for r in range(rounds):
        pl.semaphore_signal(barrier, inc=1, device_id=(ctx, partner[r]), device_id_type=MESH)

    @pl.when(has_above)
    def _():
        pl.semaphore_signal(barrier, inc=1, device_id=(above, seq), device_id_type=MESH)

    @pl.when(has_below)
    def _():
        pl.semaphore_signal(barrier, inc=1, device_id=(below, seq), device_id_type=MESH)

    pl.semaphore_wait(
        barrier, rounds + (place + n_ctx - 1) // n_ctx + (n_ctx - 1 - place + n_ctx - 1) // n_ctx
    )

    def copy(stage, c, source, device):
        return pltpu.make_async_remote_copy(
            src_ref=source,
            dst_ref=got.at[stage, c],
            send_sem=send_sem.at[stage, c],
            recv_sem=recv_sem.at[stage, c],
            device_id=device,
            device_id_type=MESH,
        )

    def exchange(r, c):
        source = x_ref.at[c] if r == 0 else tot.at[r - 1, c]
        return copy(r, c, source, (ctx, partner[r]))

    def upward(c):
        return copy(up_at, c, up.at[c], (above, seq))

    def downward(c):
        return copy(down_at, c, down.at[c], (below, seq))

    def begin(r, c):
        if r < rounds:
            if r > 0:
                exchange(r - 1, c).wait_recv()
                arrived = got[r - 1, c]
                add = jnp.where(high[r - 1] == 1, arrived, 0.0)
                if r == 1:
                    before[c] = add
                    tot[0, c] = x_ref[c] + arrived
                else:
                    before[c] += add
                    tot[r - 1, c] = tot[r - 2, c] + arrived
            exchange(r, c).start()
        elif r == rounds:
            exchange(r - 1, c).wait_recv()
            add = jnp.where(high[r - 1] == 1, got[r - 1, c], 0.0)
            before[c] = before[c] + add if rounds > 1 else add

            @pl.when(has_above & ~has_below)
            def _():
                up[c] = before[c] + x_ref[c]
                upward(c).start()

            @pl.when(has_below & ~has_above)
            def _():
                down[c] = before[c]
                downward(c).start()
        else:
            @pl.when(has_below)
            def _():
                upward(c).wait_recv()

                @pl.when(has_above)
                def _():
                    up[c] = before[c] + x_ref[c] + got[up_at, c]
                    upward(c).start()

            @pl.when(has_above)
            def _():
                downward(c).wait_recv()

                @pl.when(has_below)
                def _():
                    down[c] = before[c] + got[down_at, c]
                    downward(c).start()

            p_ref[c] = before[c]

            @pl.when(has_below)
            def _():
                p_ref[c] += got[up_at, c]

            @pl.when(has_above)
            def _():
                p_ref[c] += got[down_at, c]

    lag = 2
    for turn in range(chunks + lag * (rounds + 1)):
        for r in reversed(range(rounds + 2)):
            c = turn - lag * r
            if 0 <= c < chunks:
                begin(r, c)

    for c in range(chunks):
        for r in range(rounds):
            exchange(r, c).wait_send()

        @pl.when(has_above)
        def _():
            upward(c).wait_send()

        @pl.when(has_below)
        def _():
            downward(c).wait_send()


def scan(x, n_ctx, n_seq, reverse):
    rounds = n_seq.bit_length() - 1
    shape = x.shape
    vmem = pl.BlockSpec(memory_space=pltpu.VMEM)
    return pl.pallas_call(
        functools.partial(scan_kernel, n_ctx, n_seq, reverse),
        out_shape=jax.ShapeDtypeStruct(shape, jnp.float32),
        in_specs=[vmem],
        out_specs=vmem,
        scratch_shapes=[
            pltpu.VMEM((rounds + 2,) + shape, jnp.float32),
            pltpu.VMEM((max(rounds - 1, 1),) + shape, jnp.float32),
            pltpu.VMEM(shape, jnp.float32),
            pltpu.VMEM(shape, jnp.float32),
            pltpu.VMEM(shape, jnp.float32),
            pltpu.SemaphoreType.DMA((rounds + 2, shape[0])),
            pltpu.SemaphoreType.DMA((rounds + 2, shape[0])),
        ],
        compiler_params=pltpu.CompilerParams(
            collective_id=1 if reverse else 0,
            has_side_effects=True,
            vmem_limit_bytes=48 << 20,
        ),
        name="scan_later" if reverse else "scan_earlier",
    )(x)


def per_device(n_ctx, n_seq, queries, keys, values, grad_output):
    length = queries.shape[0]
    pick_a, pick_b, aux, aux_column = tables()
    whole = pl.BlockSpec((length, LANES), lambda h: (0, 0))
    wide = pl.BlockSpec((length, HEAD_DIM), lambda h: (0, h))
    state = pl.BlockSpec((1, ROWS, HEAD_DIM), lambda h: (h, 0, 0))
    pick = pl.BlockSpec((1, ROWS, LANES), lambda h: (h, 0, 0))
    row = pl.BlockSpec((8, ROWS), lambda h: (0, 0))
    column = pl.BlockSpec((ROWS, LANES), lambda h: (0, 0))
    params = pltpu.CompilerParams(
        dimension_semantics=("arbitrary",), vmem_limit_bytes=48 << 20
    )
    state_shape = jax.ShapeDtypeStruct((HEADS, ROWS, HEAD_DIM), jnp.float32)
    narrow_acc = pltpu.VMEM((length, LANES), jnp.float32)
    f32, bf16 = jnp.float32, jnp.bfloat16

    mine = pl.pallas_call(
        key_state_kernel,
        grid=(HEADS,),
        out_shape=state_shape,
        in_specs=[whole, wide, pick, pick, column],
        out_specs=state,
        compiler_params=params,
        name="key_state",
    )(keys, values, pick_a, pick_b, aux_column)
    prior = scan(mine, n_ctx, n_seq, False)
    attended, grad_query, terms, key_part, value_part = pl.pallas_call(
        middle_kernel,
        grid=(HEADS,),
        out_shape=(
            jax.ShapeDtypeStruct(values.shape, bf16),
            jax.ShapeDtypeStruct(queries.shape, bf16),
            state_shape,
            jax.ShapeDtypeStruct(keys.shape, f32),
            jax.ShapeDtypeStruct(values.shape, f32),
        ),
        in_specs=[whole, whole, wide, wide, state, pick, pick, row, column],
        out_specs=(wide, whole, state, whole, wide),
        scratch_shapes=[narrow_acc, narrow_acc],
        compiler_params=params,
        name="middle",
    )(queries, keys, values, grad_output, prior, pick_a, pick_b, aux, aux_column)
    later = scan(terms, n_ctx, n_seq, True)
    grad_key, grad_value = pl.pallas_call(
        last_kernel,
        grid=(HEADS,),
        out_shape=(
            jax.ShapeDtypeStruct(keys.shape, bf16),
            jax.ShapeDtypeStruct(values.shape, bf16),
        ),
        in_specs=[whole, wide, state, whole, wide, pick, pick, row],
        out_specs=(whole, wide),
        scratch_shapes=[narrow_acc],
        compiler_params=params,
        name="last",
    )(keys, values, later, key_part, value_part, pick_a, pick_b, aux)
    return attended, grad_query, grad_key, grad_value


def solution(mesh):
    placed = P(("seq", "ctx"), None)
    return jax.shard_map(
        functools.partial(per_device, mesh.shape["ctx"], mesh.shape["seq"]),
        mesh=mesh,
        in_specs=(placed,) * 4,
        out_specs=(placed,) * 4,
        check_vma=False,
    )
```

time: 404 us -> 179 us (0.44)
  waiting for transfers between devices: 178 us -> 0 us
  Pallas kernels: 0 us -> 172 us
  blocking collectives: 78.5 us -> 0 us
  other arithmetic: 55.9 us -> 0 us
  local copies, waits for them, and re-layouts: 39.8 us -> 4.74 us
  matrix products: 33.9 us -> 0 us
  between operations: 14.7 us -> 0.76 us
    pallas_call x0 -> x5, Pallas kernels: none -> 172 us  [the longest x2 145 us: scan(): pl.pallas_call(functools.partial(scan_kernel, n_ctx, n_seq, reverse), out...]
    psum x2 -> x0, waiting for transfers between devices: 96.5 us -> none  [combine(): total = lax.psum((pair[0], pair[1]), 'ctx')]
    all_gather x4 -> x0, waiting for transfers between devices: 79.1 us -> none  [carried_in(): gathered = jax.tree.map(lambda a: lax.all_gather(a, axis), part)]
    all_gather x4 -> x0, blocking collectives: 57 us -> none  [carried_in(): gathered = jax.tree.map(lambda a: lax.all_gather(a, axis), part)]
    scatter-add x4 -> x0, other arithmetic: 41.7 us -> none  [the longest x2 23.5 us: features(): entries[:, lower, :]]
    dot_general x14 -> x0, matrix products: 33.9 us -> none  [the longest x1 3.73 us: per_device(): jnp.einsum('hfe,the->hft', prior_state, scaled, precision=HIGHEST)]
    psum x2 -> x0, blocking collectives: 21.5 us -> none  [combine(): total = lax.psum((pair[0], pair[1]), 'ctx')]
    dynamic_slice x10 -> x0, local copies, waits for them, and re-layouts: 11.4 us -> none  [one(): lax.dynamic_index_in_dim(a, source, 0, False)]
  transfers between devices with their start and end apart: 6 -> 0, of which waited for: 5 -> 0; matrix products, arithmetic and copies ran while one was open for 8% -> 0% of each run, Pallas kernels for 0% -> 0%
where the time goes in v1:
time: 179 us; the launch traced here: 178 us
  Pallas kernels  172 us (96%)
  local copies, waits for them, and re-layouts  4.74 us (3%)
    pallas_call x2, Pallas kernels, scan(): pl.pallas_call(functools.partial(scan_kernel, n_ctx, n_seq, reverse), out...  145 us
    pallas_call x1, Pallas kernels, per_device(): pl.pallas_call(middle_kernel, grid=(HEADS,), out_shape=(jax.ShapeDtypeStr...  15 us
    pallas_call x1, Pallas kernels, per_device(): pl.pallas_call(last_kernel, grid=(HEADS,), out_shape=(jax.ShapeDtypeStruc...  8.98 us
    unnamed x22, local copies, waits for them, and re-layouts  4.74 us

profile of v1, /device:TPU:0, one launch (start us, length us, event | category | flops | bytes accessed | tf_op | source)
XLA Modules:
  0.0 177.8 jit_solution(9263896247990659792)
XLA Ops:
  0.6 0.0 copy-start
  0.6 1.0 copy-done
  1.7 0.0 copy-start.2
  1.7 1.0 copy-done.2
  2.6 0.0 copy-start.4
  2.7 1.0 copy-done.4
  3.6 0.0 copy-start.6
  3.6 0.8 copy-done.6
  4.5 0.0 copy-start.8
  4.5 0.9 copy-done.8
  5.3 0.0 copy-start.7
  5.4 3.0 %key_state.1.x_ref = f32[8,160,128]{2,1,0:T(8,128)S(1)} custom-call(bf16[256,128]{1,0:T(8,128)(2,1)S(1)} %copy-done.6, bf16[256,1024]{1,0:T(8,128)(2,1)S(1)} %copy-done, bf16[8,160,128]{2,1,0:T(8,128)(2,1)S(1)} %copy-done.4, bf16[8,160,128]{2,1,0:T(8,128)(2,1)S(1)} %copy-done.2, f32[160,128]{1,0:T(8,128)S(1)} %copy-done.8), custom_call_target="tpu_custom_call" | custom-call | tf_op jit(solution)/shard_map/key_state/pallas_call | solution.py:372
  8.3 0.0 copy-start.1
  8.4 0.0 copy-start.3
  8.4 0.0 copy-start.5
  8.4 0.0 copy-start.9
  8.4 0.0 copy-start.10
  8.4 78.0 %scan_earlier.1.p_ref = f32[8,160,128]{2,1,0:T(8,128)S(1)} custom-call(f32[8,160,128]{2,1,0:T(8,128)S(1)} %key_state.1.x_ref), custom_call_target="tpu_custom_call" | custom-call | tf_op jit(solution)/shard_map/scan_earlier/pallas_call | solution.py:333
  86.5 0.0 copy-done.7
  86.5 0.0 copy-done.1
  86.5 0.0 copy-done.3
  86.5 0.0 copy-done.5
  86.5 0.0 copy-done.9
  86.5 0.0 copy-done.10
  86.5 15.0 %middle.1 = (bf16[256,1024]{1,0:T(8,128)(2,1)}, bf16[256,128]{1,0:T(8,128)(2,1)}, f32[8,160,128]{2,1,0:T(8,128)S(1)}, f32[256,128]{1,0:T(8,128)S(1)}, f32[256,1024]{1,0:T(8,128)S(1)}) custom-call(bf16[256,128]{1,0:T(8,128)(2,1)S(1)} %copy-done.9, bf16[256,128]{1,0:T(8,128)(2,1)S(1)} %copy-done.6, bf16[256,1024]{1,0:T(8,128)(2,1)S(1)} %copy-done.1, ...), custom_call_target="tpu_custom_call" | custom-call | tf_op jit(solution)/shard_map/middle/pallas_call | solution.py:382
  101.5 67.3 %scan_later.1.l_ref = f32[8,160,128]{2,1,0:T(8,128)S(1)} custom-call(f32[8,160,128]{2,1,0:T(8,128)S(1)} %get-tuple-element.13.x_ref), custom_call_target="tpu_custom_call" | custom-call | tf_op jit(solution)/shard_map/scan_later/pallas_call | solution.py:333
  168.8 9.0 %last.1 = (bf16[256,128]{1,0:T(8,128)(2,1)}, bf16[256,1024]{1,0:T(8,128)(2,1)}) custom-call(bf16[256,128]{1,0:T(8,128)(2,1)S(1)} %copy-done.6, bf16[256,1024]{1,0:T(8,128)(2,1)S(1)} %copy-done.1, f32[8,160,128]{2,1,0:T(8,128)S(1)} %scan_later.1.l_ref, f32[256,128]{1,0:T(8,128)S(1)} %get-tuple-element.14.gk_in, f32[256,1024]{1,0:T(8,128)S(1)} %get-tuple-element.15.gv_in, ...), custom_call_target="tpu_custom_call" | custom-call | tf_op jit(solution)/shard_map/last/pallas_call | solution.py:399
Async XLA Ops:
  0.6 1.0 copy-start
  1.7 1.0 copy-start.2
  2.6 1.0 copy-start.4
  3.6 0.8 copy-start.6
  4.5 0.9 copy-start.8
  5.3 81.1 %copy-start.7 = (bf16[256,1024]{1,0:T(8,128)(2,1)S(1)}, bf16[256,1024]{1,0:T(8,128)(2,1)}, u32[]{:S(2)}) copy-start(bf16[256,1024]{1,0:T(8,128)(2,1)} %g_ref.1) | copy-start | bytes 1572868
  8.3 78.1 %copy-start.1 = (bf16[256,1024]{1,0:T(8,128)(2,1)S(1)}, bf16[256,1024]{1,0:T(8,128)(2,1)}, u32[]{:S(2)}) copy-start(bf16[256,1024]{1,0:T(8,128)(2,1)} %v_ref.5) | copy-start | bytes 1572868
  8.4 78.1 %copy-start.3 = (bf16[8,160,128]{2,1,0:T(8,128)(2,1)S(1)}, bf16[8,160,128]{2,1,0:T(8,128)(2,1)}, u32[]{:S(2)}) copy-start(bf16[8,160,128]{2,1,0:T(8,128)(2,1)} %constant.9.clone.b_ref) | copy-start | bytes 983044
  8.4 78.1 %copy-start.5 = (bf16[8,160,128]{2,1,0:T(8,128)(2,1)S(1)}, bf16[8,160,128]{2,1,0:T(8,128)(2,1)}, u32[]{:S(2)}) copy-start(bf16[8,160,128]{2,1,0:T(8,128)(2,1)} %constant.8.clone.a_ref) | copy-start | bytes 983044
  8.4 78.1 %copy-start.9 = (bf16[256,128]{1,0:T(8,128)(2,1)S(1)}, bf16[256,128]{1,0:T(8,128)(2,1)}, u32[]{:S(2)}) copy-start(bf16[256,128]{1,0:T(8,128)(2,1)} %q_ref.1) | copy-start | bytes 196612
  8.4 78.1 %copy-start.10 = (f32[8,160]{1,0:T(8,128)S(1)}, f32[8,160]{1,0:T(8,128)}, u32[]{:S(2)}) copy-start(f32[8,160]{1,0:T(8,128)} %constant.10.clone.aux_ref) | copy-start | bytes 15364

commit v2 on v1

--- a/solution.py
+++ b/solution.py
@@ -194,12 +194,13 @@
 
 
 def scan_kernel(
-    n_ctx, n_seq, reverse, x_ref, p_ref, got, tot, before, up, down,
-    send_sem, recv_sem,
+    n_ctx, n_seq, reverse, lags, x_ref, p_ref, peer, other, got, tot, part, before, up_got, up,
+    down_got, down, send_sem, recv_sem,
 ):
+    pair_lag, round_lag, share_lag, hop_lag = lags
     rounds = n_seq.bit_length() - 1
-    chunks = x_ref.shape[0]
-    up_at, down_at = rounds, rounds + 1
+    chunks, _, rows, _ = x_ref.shape
+    share_at, up_at, down_at = rounds, rounds + 1, rounds + 2
     ctx, seq = lax.axis_index("ctx"), lax.axis_index("seq")
     if reverse:
         place, line = n_ctx - 1 - ctx, n_seq - 1 - seq
@@ -209,6 +210,8 @@
         step = 1
     high = [(line // (1 << r)) % 2 for r in range(rounds)]
     partner = [seq + step * (1 << r) * (1 - 2 * high[r]) for r in range(rounds)]
+    mine = high[0]
+    theirs = 1 - mine
     has_above = place < n_ctx - 1
     has_below = place > 0
     above = lax.rem(ctx + step + n_ctx, n_ctx)
@@ -230,119 +233,156 @@
         barrier, rounds + (place + n_ctx - 1) // n_ctx + (n_ctx - 1 - place + n_ctx - 1) // n_ctx
     )
 
-    def copy(stage, c, source, device):
+    def copy(stage, c, source, target, device):
         return pltpu.make_async_remote_copy(
             src_ref=source,
-            dst_ref=got.at[stage, c],
+            dst_ref=target,
             send_sem=send_sem.at[stage, c],
             recv_sem=recv_sem.at[stage, c],
             device_id=device,
             device_id_type=MESH,
         )
 
+    def swap(c):
+        return copy(0, c, x_ref.at[c], peer.at[c], (ctx, partner[0]))
+
     def exchange(r, c):
-        source = x_ref.at[c] if r == 0 else tot.at[r - 1, c]
-        return copy(r, c, source, (ctx, partner[r]))
+        return copy(r, c, tot.at[r - 1, c], got.at[r - 1, c], (ctx, partner[r]))
+
+    def share(c):
+        return copy(share_at, c, part.at[c], other.at[c], (ctx, partner[0]))
 
     def upward(c):
-        return copy(up_at, c, up.at[c], (above, seq))
+        return copy(up_at, c, up.at[c], up_got.at[c], (above, seq))
 
     def downward(c):
-        return copy(down_at, c, down.at[c], (below, seq))
-
-    def begin(r, c):
-        if r < rounds:
-            if r > 0:
-                exchange(r - 1, c).wait_recv()
-                arrived = got[r - 1, c]
-                add = jnp.where(high[r - 1] == 1, arrived, 0.0)
-                if r == 1:
-                    before[c] = add
-                    tot[0, c] = x_ref[c] + arrived
-                else:
-                    before[c] += add
-                    tot[r - 1, c] = tot[r - 2, c] + arrived
-            exchange(r, c).start()
-        elif r == rounds:
-            exchange(r - 1, c).wait_recv()
-            add = jnp.where(high[r - 1] == 1, got[r - 1, c], 0.0)
-            before[c] = before[c] + add if rounds > 1 else add
-
-            @pl.when(has_above & ~has_below)
+        return copy(down_at, c, down.at[c], down_got.at[c], (below, seq))
+
+    def first(c):
+        swap(c).wait_recv()
+        tot[0, c] = x_ref[c, mine] + peer[c, mine]
+        exchange(1, c).start()
+
+    def middle(r, c):
+        exchange(r, c).wait_recv()
+        arrived = got[r - 1, c]
+        add = jnp.where(high[r] == 1, arrived, 0.0)
+        part[c] = add if r == 1 else part[c] + add
+        if r < rounds - 1:
+            tot[r, c] = tot[r - 1, c] + arrived
+            exchange(r + 1, c).start()
+        else:
+            share(c).start()
+
+    def joined(c):
+        share(c).wait_recv()
+        before[c, mine] = part[c] + jnp.where(mine == 1, peer[c, mine], 0.0)
+        before[c, theirs] = other[c] + jnp.where(mine == 1, peer[c, theirs], 0.0)
+
+        @pl.when(has_above & ~has_below)
+        def _():
+            up[c] = before[c] + x_ref[c]
+            upward(c).start()
+
+        @pl.when(has_below & ~has_above)
+        def _():
+            down[c] = before[c]
+            downward(c).start()
+
+    def rise(c):
+        upward(c).wait_recv()
+
+        @pl.when(has_above)
+        def _():
+            up[c] = before[c] + x_ref[c] + up_got[c]
+            upward(c).start()
+
+    def sink(c):
+        downward(c).wait_recv()
+
+        @pl.when(has_below)
+        def _():
+            down[c] = before[c] + down_got[c]
+            downward(c).start()
+
+    for c in range(chunks):
+        swap(c).start()
+
+    stages = [(first, pair_lag)]
+    at = pair_lag
+    for r in range(1, rounds):
+        at += round_lag
+        stages.append((functools.partial(middle, r), at))
+    at += share_lag
+    stages.append((joined, at))
+    turns = at + hop_lag * (n_ctx - 1) + chunks
+    rise_at = at + hop_lag * place
+    sink_at = at + hop_lag * (n_ctx - 1 - place)
+
+    def turn(t, _):
+        def run(body, start, extra=None):
+            c = t - start
+            ok = (c >= 0) & (c < chunks)
+
+            @pl.when(ok if extra is None else ok & extra)
             def _():
-                up[c] = before[c] + x_ref[c]
-                upward(c).start()
-
-            @pl.when(has_below & ~has_above)
-            def _():
-                down[c] = before[c]
-                downward(c).start()
-        else:
-            @pl.when(has_below)
-            def _():
-                upward(c).wait_recv()
-
-                @pl.when(has_above)
-                def _():
-                    up[c] = before[c] + x_ref[c] + got[up_at, c]
-                    upward(c).start()
-
-            @pl.when(has_above)
-            def _():
-                downward(c).wait_recv()
-
-                @pl.when(has_below)
-                def _():
-                    down[c] = before[c] + got[down_at, c]
-                    downward(c).start()
-
-            p_ref[c] = before[c]
-
-            @pl.when(has_below)
-            def _():
-                p_ref[c] += got[up_at, c]
-
-            @pl.when(has_above)
-            def _():
-                p_ref[c] += got[down_at, c]
-
-    lag = 2
-    for turn in range(chunks + lag * (rounds + 1)):
-        for r in reversed(range(rounds + 2)):
-            c = turn - lag * r
-            if 0 <= c < chunks:
-                begin(r, c)
-
-    for c in range(chunks):
-        for r in range(rounds):
+                body(c)
+
+        run(sink, sink_at, has_above)
+        run(rise, rise_at, has_below)
+        for body, start in reversed(stages):
+            run(body, start)
+        return 0
+
+    lax.fori_loop(pair_lag, turns, turn, 0)
+
+    def finish(c, _):
+        p_ref[c] = before[c]
+
+        @pl.when(has_below)
+        def _():
+            p_ref[c] += up_got[c]
+            downward(c).wait_send()
+
+        @pl.when(has_above)
+        def _():
+            p_ref[c] += down_got[c]
+            upward(c).wait_send()
+
+        swap(c).wait_send()
+        for r in range(1, rounds):
             exchange(r, c).wait_send()
-
-        @pl.when(has_above)
-        def _():
-            upward(c).wait_send()
-
-        @pl.when(has_below)
-        def _():
-            downward(c).wait_send()
-
-
-def scan(x, n_ctx, n_seq, reverse):
+        share(c).wait_send()
+        return 0
+
+    lax.fori_loop(0, chunks, finish, 0)
+
+
+def scan(x, n_ctx, n_seq, reverse, chunks=8, lags=(1, 2, 1, 2)):
     rounds = n_seq.bit_length() - 1
-    shape = x.shape
+    rows = x.shape[0] * x.shape[1] // (2 * chunks)
+    full = (chunks, 2, rows, 128)
+    half = (chunks, rows, 128)
     vmem = pl.BlockSpec(memory_space=pltpu.VMEM)
+    f32 = jnp.float32
     return pl.pallas_call(
-        functools.partial(scan_kernel, n_ctx, n_seq, reverse),
-        out_shape=jax.ShapeDtypeStruct(shape, jnp.float32),
+        functools.partial(scan_kernel, n_ctx, n_seq, reverse, lags),
+        out_shape=jax.ShapeDtypeStruct(full, f32),
         in_specs=[vmem],
         out_specs=vmem,
         scratch_shapes=[
-            pltpu.VMEM((rounds + 2,) + shape, jnp.float32),
-            pltpu.VMEM((max(rounds - 1, 1),) + shape, jnp.float32),
-            pltpu.VMEM(shape, jnp.float32),
-            pltpu.VMEM(shape, jnp.float32),
-            pltpu.VMEM(shape, jnp.float32),
-            pltpu.SemaphoreType.DMA((rounds + 2, shape[0])),
-            pltpu.SemaphoreType.DMA((rounds + 2, shape[0])),
+            pltpu.VMEM(full, f32),
+            pltpu.VMEM(half, f32),
+            pltpu.VMEM((rounds - 1,) + half, f32),
+            pltpu.VMEM((rounds - 1,) + half, f32),
+            pltpu.VMEM(half, f32),
+            pltpu.VMEM(full, f32),
+            pltpu.VMEM(full, f32),
+            pltpu.VMEM(full, f32),
+            pltpu.VMEM(full, f32),
+            pltpu.VMEM(full, f32),
+            pltpu.SemaphoreType.DMA((rounds + 3, chunks)),
+            pltpu.SemaphoreType.DMA((rounds + 3, chunks)),
         ],
         compiler_params=pltpu.CompilerParams(
             collective_id=1 if reverse else 0,
@@ -350,7 +390,7 @@
             vmem_limit_bytes=48 << 20,
         ),
         name="scan_later" if reverse else "scan_earlier",
-    )(x)
+    )(x.reshape(full)).reshape(x.shape)
 
 
 def per_device(n_ctx, n_seq, queries, keys, values, grad_output):

time: 179 us -> 106 us (0.59)
  Pallas kernels: 172 us -> 100 us
    pallas_call x2, Pallas kernels: 145 us -> 73.3 us  [scan(): pl.pallas_call(functools.partial(scan_kernel, n_ctx, n_seq, reverse, lags...]
where the time goes in v2:
time: 106 us
  Pallas kernels  100 us (94%)
  local copies, waits for them, and re-layouts  4.74 us (4%)
    pallas_call x2, Pallas kernels, scan(): pl.pallas_call(functools.partial(scan_kernel, n_ctx, n_seq, reverse, lags...  73.3 us
    pallas_call x1, Pallas kernels, per_device(): pl.pallas_call(middle_kernel, grid=(HEADS,), out_shape=(jax.ShapeDtypeStr...  15 us
    pallas_call x1, Pallas kernels, per_device(): pl.pallas_call(last_kernel, grid=(HEADS,), out_shape=(jax.ShapeDtypeStruc...  8.97 us
    unnamed x22, local copies, waits for them, and re-layouts  4.74 us
    pallas_call x1, Pallas kernels, per_device(): pl.pallas_call(key_state_kernel, grid=(HEADS,), out_shape=state_shape, in...  2.99 us

profile of v2, /device:TPU:0, one launch (start us, length us, event | category | flops | bytes accessed | tf_op | source)
XLA Modules:
  0.0 105.7 jit_solution(1607334951437268524)
XLA Ops:
  0.6 0.0 copy-start
  0.6 1.0 copy-done
  1.7 0.0 copy-start.2
  1.7 1.0 copy-done.2
  2.6 0.0 copy-start.4
  2.7 1.0 copy-done.4
  3.6 0.0 copy-start.6
  3.6 0.8 copy-done.6
  4.5 0.0 copy-start.8
  4.5 0.9 copy-done.8
  5.3 0.0 copy-start.7
  5.4 3.0 %key_state.1 = f32[8,160,128]{2,1,0:T(8,128)S(1)} custom-call(bf16[256,128]{1,0:T(8,128)(2,1)S(1)} %copy-done.6, bf16[256,1024]{1,0:T(8,128)(2,1)S(1)} %copy-done, bf16[8,160,128]{2,1,0:T(8,128)(2,1)S(1)} %copy-done.4, bf16[8,160,128]{2,1,0:T(8,128)(2,1)S(1)} %copy-done.2, f32[160,128]{1,0:T(8,128)S(1)} %copy-done.8), custom_call_target="tpu_custom_call" | custom-call | tf_op jit(solution)/shard_map/key_state/pallas_call | solution.py:412
  8.3 0.0 copy-start.1
  8.4 0.0 copy-start.3
  8.4 0.0 copy-start.5
  8.4 0.0 copy-start.9
  8.4 0.0 copy-start.10
  8.4 37.9 %scan_earlier.1 = f32[8,2,80,128]{3,2,1,0:T(8,128)S(1)} custom-call(f32[8,2,80,128]{3,2,1,0:T(8,128)S(1)} %bitcast.5), custom_call_target="tpu_custom_call" | custom-call | tf_op jit(solution)/shard_map/scan_earlier/pallas_call | solution.py:368
  46.3 0.0 copy-done.7
  46.4 0.0 copy-done.1
  46.4 0.0 copy-done.3
  46.4 0.0 copy-done.5
  46.4 0.0 copy-done.9
  46.4 0.0 copy-done.10
  46.4 15.0 %middle.1 = (bf16[256,1024]{1,0:T(8,128)(2,1)}, bf16[256,128]{1,0:T(8,128)(2,1)}, f32[8,160,128]{2,1,0:T(8,128)S(1)}, f32[256,128]{1,0:T(8,128)S(1)}, f32[256,1024]{1,0:T(8,128)S(1)}) custom-call(bf16[256,128]{1,0:T(8,128)(2,1)S(1)} %copy-done.9, bf16[256,128]{1,0:T(8,128)(2,1)S(1)} %copy-done.6, bf16[256,1024]{1,0:T(8,128)(2,1)S(1)} %copy-done.1, ...), custom_call_target="tpu_custom_call" | custom-call | tf_op jit(solution)/shard_map/middle/pallas_call | solution.py:422
  61.4 35.4 %scan_later.1 = f32[8,2,80,128]{3,2,1,0:T(8,128)S(1)} custom-call(f32[8,2,80,128]{3,2,1,0:T(8,128)S(1)} %bitcast.7), custom_call_target="tpu_custom_call" | custom-call | tf_op jit(solution)/shard_map/scan_later/pallas_call | solution.py:368
  96.8 9.0 %last.1 = (bf16[256,128]{1,0:T(8,128)(2,1)}, bf16[256,1024]{1,0:T(8,128)(2,1)}) custom-call(bf16[256,128]{1,0:T(8,128)(2,1)S(1)} %copy-done.6, bf16[256,1024]{1,0:T(8,128)(2,1)S(1)} %copy-done.1, f32[8,160,128]{2,1,0:T(8,128)S(1)} %bitcast.6, f32[256,128]{1,0:T(8,128)S(1)} %get-tuple-element.14.gk_in, f32[256,1024]{1,0:T(8,128)S(1)} %get-tuple-element.15.gv_in, ...), custom_call_target="tpu_custom_call" | custom-call | tf_op jit(solution)/shard_map/last/pallas_call | solution.py:439
Async XLA Ops:
  0.6 1.0 copy-start
  1.7 1.0 copy-start.2
  2.6 1.0 copy-start.4
  3.6 0.8 copy-start.6
  4.5 0.9 copy-start.8
  5.3 41.0 %copy-start.7 = (bf16[256,1024]{1,0:T(8,128)(2,1)S(1)}, bf16[256,1024]{1,0:T(8,128)(2,1)}, u32[]{:S(2)}) copy-start(bf16[256,1024]{1,0:T(8,128)(2,1)} %g_ref.1) | copy-start | bytes 1572868
  8.3 38.0 %copy-start.1 = (bf16[256,1024]{1,0:T(8,128)(2,1)S(1)}, bf16[256,1024]{1,0:T(8,128)(2,1)}, u32[]{:S(2)}) copy-start(bf16[256,1024]{1,0:T(8,128)(2,1)} %v_ref.5) | copy-start | bytes 1572868
  8.4 38.0 %copy-start.3 = (bf16[8,160,128]{2,1,0:T(8,128)(2,1)S(1)}, bf16[8,160,128]{2,1,0:T(8,128)(2,1)}, u32[]{:S(2)}) copy-start(bf16[8,160,128]{2,1,0:T(8,128)(2,1)} %constant.9.clone.b_ref) | copy-start | bytes 983044
  8.4 38.0 %copy-start.5 = (bf16[8,160,128]{2,1,0:T(8,128)(2,1)S(1)}, bf16[8,160,128]{2,1,0:T(8,128)(2,1)}, u32[]{:S(2)}) copy-start(bf16[8,160,128]{2,1,0:T(8,128)(2,1)} %constant.8.clone.a_ref) | copy-start | bytes 983044
  8.4 38.0 %copy-start.9 = (bf16[256,128]{1,0:T(8,128)(2,1)S(1)}, bf16[256,128]{1,0:T(8,128)(2,1)}, u32[]{:S(2)}) copy-start(bf16[256,128]{1,0:T(8,128)(2,1)} %q_ref.1) | copy-start | bytes 196612
  8.4 38.0 %copy-start.10 = (f32[8,160]{1,0:T(8,128)S(1)}, f32[8,160]{1,0:T(8,128)}, u32[]{:S(2)}) copy-start(f32[8,160]{1,0:T(8,128)} %constant.10.clone.aux_ref) | copy-start | bytes 15364

commit v3 on v0

v3 whole, which is shorter than its diff:
```python
import functools
import math

import jax
import jax.numpy as jnp
import numpy as np
from jax import lax
from jax.experimental import pallas as pl
from jax.experimental.pallas import tpu as pltpu
from jax.sharding import PartitionSpec as P

HEADS = 8
QK_DIM = 16
HEAD_DIM = 128
FEATURES = 153
ROWS = 160
LANES = 128
MESH = pl.DeviceIdType.MESH
NN = (((1,), (0,)), ((), ()))
NT = (((1,), (1,)), ((), ()))
TN = (((0,), (0,)), ((), ()))


def tables():
    upper, lower = np.triu_indices(QK_DIM)
    pick_a = np.zeros((HEADS, ROWS, LANES), np.float32)
    pick_b = np.zeros((HEADS, ROWS, LANES), np.float32)
    aux = np.zeros((8, ROWS), np.float32)
    aux[0, 0] = 1.0
    aux[1, : 1 + QK_DIM] = 1.0
    aux[2, 0] = 1.0
    aux[2, 1 : 1 + QK_DIM] = 1.0 / math.sqrt(math.sqrt(QK_DIM))
    aux[2, 1 + QK_DIM : FEATURES] = np.where(upper == lower, 1.0, math.sqrt(2.0)) / math.sqrt(
        2.0 * QK_DIM
    )
    for head in range(HEADS):
        base = head * QK_DIM
        for i in range(QK_DIM):
            pick_a[head, 1 + i, base + i] = 1.0
        for n, (i, j) in enumerate(zip(upper, lower)):
            pick_a[head, 1 + QK_DIM + n, base + i] = 1.0
            pick_b[head, 1 + QK_DIM + n, base + j] = 1.0
    aux_column = np.zeros((ROWS, LANES), np.float32)
    aux_column[:, :8] = aux.T
    return (
        jnp.asarray(pick_a, jnp.bfloat16),
        jnp.asarray(pick_b, jnp.bfloat16),
        jnp.asarray(aux),
        jnp.asarray(aux_column),
    )


def dot(a, b, dims=NN):
    return lax.dot_general(a, b, dims, preferred_element_type=jnp.float32)


def split(x):
    high = x.astype(jnp.bfloat16)
    return high, (x - high.astype(jnp.float32)).astype(jnp.bfloat16)


def dot2(pair, b, dims=NN):
    return dot(pair[0], b, dims) + dot(pair[1], b, dims)


def dot2r(a, pair, dims=NN):
    return dot(a, pair[0], dims) + dot(a, pair[1], dims)


def dot3(x, y, dims=NN):
    return dot(x[0], y[0], dims) + (dot(x[0], y[1], dims) + dot(x[1], y[0], dims))


def features_by_row(pick_a, pick_b, aux_column, x):
    a = dot(pick_a, x, NT) + aux_column[:, 0:1]
    b = dot(pick_b, x, NT) + aux_column[:, 1:2]
    return a * b * aux_column[:, 2:3]


def factors_by_token(pick_a, pick_b, aux, x):
    a = dot(x, pick_a, NT) + aux[0:1, :]
    b = dot(x, pick_b, NT) + aux[1:2, :]
    return a, b


def put_state(ref, head, state, norm):
    ref[head] = state.reshape(2, ROWS // 2, LANES)
    row = FEATURES - ROWS // 2
    ref[head, 1, row : row + 1, :] = norm[0:1, :LANES]
    ref[head, 1, row + 1 : row + 2, : ROWS - LANES] = norm[0:1, LANES:ROWS]


def norm_of(state):
    return jnp.concatenate(
        [state[FEATURES : FEATURES + 1, :], state[FEATURES + 1 : FEATURES + 2, : ROWS - LANES]],
        axis=1,
    )


def pull(grad, a, b, pick_a, pick_b):
    return dot2(split(grad * b), pick_a) + dot2(split(grad * a), pick_b)


class Scan:
    def __init__(self, n_ctx, n_seq, reverse, refs):
        (
            self.x, self.peer, self.other, self.got, self.tot, self.part, self.before,
            self.up_got, self.up, self.down_got, self.down, self.send_sem, self.recv_sem,
        ) = refs
        self.rounds = n_seq.bit_length() - 1
        ctx, seq = lax.axis_index("ctx"), lax.axis_index("seq")
        step = -1 if reverse else 1
        self.n_ctx = n_ctx
        self.place = n_ctx - 1 - ctx if reverse else ctx
        line = n_seq - 1 - seq if reverse else seq
        self.high = [(line // (1 << r)) % 2 for r in range(self.rounds)]
        self.partner = [
            (ctx, seq + step * (1 << r) * (1 - 2 * self.high[r])) for r in range(self.rounds)
        ]
        self.mine = self.high[0]
        self.has_above = self.place < n_ctx - 1
        self.has_below = self.place > 0
        self.above = (lax.rem(ctx + step + n_ctx, n_ctx), seq)
        self.below = (lax.rem(ctx - step + n_ctx, n_ctx), seq)

    def copy(self, stage, c, source, target, device):
        return pltpu.make_async_remote_copy(
            src_ref=source,
            dst_ref=target,
            send_sem=self.send_sem.at[stage, c],
            recv_sem=self.recv_sem.at[stage, c],
            device_id=device,
            device_id_type=MESH,
        )

    def swap(self, c):
        return self.copy(0, c, self.x.at[c], self.peer.at[c], self.partner[0])

    def exchange(self, r, c):
        return self.copy(r, c, self.tot.at[r - 1, c], self.got.at[r - 1, c], self.partner[r])

    def share(self, c):
        return self.copy(
            self.rounds, c, self.part.at[c], self.other.at[c], self.partner[0]
        )

    def upward(self, c):
        return self.copy(self.rounds + 1, c, self.up.at[c], self.up_got.at[c], self.above)

    def downward(self, c):
        return self.copy(self.rounds + 2, c, self.down.at[c], self.down_got.at[c], self.below)

    def first(self, c):
        self.swap(c).wait_recv()
        self.tot[0, c] = self.x[c, self.mine] + self.peer[c, self.mine]
        self.exchange(1, c).start()

    def round(self, r, c):
        self.exchange(r, c).wait_recv()
        arrived = self.got[r - 1, c]
        add = jnp.where(self.high[r] == 1, arrived, 0.0)
        self.part[c] = add if r == 1 else self.part[c] + add
        if r < self.rounds - 1:
            self.tot[r, c] = self.tot[r - 1, c] + arrived
            self.exchange(r + 1, c).start()
        else:
            self.share(c).start()

    def joined(self, c):
        self.share(c).wait_recv()
        mine = self.mine
        for half, value in ((mine, self.part[c]), (1 - mine, self.other[c])):
            self.before[c, half] = value + jnp.where(mine == 1, self.peer[c, half], 0.0)

        @pl.when(self.has_above & ~self.has_below)
        def _():
            self.up[c] = self.before[c] + self.x[c]
            self.upward(c).start()

        @pl.when(self.has_below & ~self.has_above)
        def _():
            self.down[c] = self.before[c]
            self.downward(c).start()

    def rise(self, c):
        self.upward(c).wait_recv()

        @pl.when(self.has_above)
        def _():
            self.up[c] = self.before[c] + self.x[c] + self.up_got[c]
            self.upward(c).start()

    def sink(self, c):
        self.downward(c).wait_recv()

        @pl.when(self.has_below)
        def _():
            self.down[c] = self.before[c] + self.down_got[c]
            self.downward(c).start()

    def result(self, c):
        total = self.before[c]
        total = total + jnp.where(self.has_below, self.up_got[c], 0.0)
        total = total + jnp.where(self.has_above, self.down_got[c], 0.0)
        return total.reshape(ROWS, LANES)

    def stages(self, start, lags):
        pair_lag, round_lag, share_lag, hop_lag = lags
        at = start + pair_lag
        out = [(self.first, at, None)]
        for r in range(1, self.rounds):
            at += round_lag
            out.append((functools.partial(self.round, r), at, None))
        at += share_lag
        out.append((self.joined, at, None))
        out.append((self.rise, at + hop_lag * self.place, self.has_below))
        out.append((self.sink, at + hop_lag * (self.n_ctx - 1 - self.place), self.has_above))
        return out, at + hop_lag * (self.n_ctx - 1)

    def finish(self, c):
        self.swap(c).wait_send()
        for r in range(1, self.rounds):
            self.exchange(r, c).wait_send()
        self.share(c).wait_send()

        @pl.when(self.has_below)
        def _():
            self.downward(c).wait_send()

        @pl.when(self.has_above)
        def _():
            self.upward(c).wait_send()


def kernel(
    n_ctx, n_seq, lags, q_ref, k_ref, v_ref, g_ref, a_ref, b_ref, aux_ref, auxc_ref,
    out_ref, gq_ref, gk_ref, gv_ref, gq_acc, gk_acc, gv_acc, *refs,
):
    count = len(refs) // 2
    earlier = Scan(n_ctx, n_seq, False, refs[:count])
    later = Scan(n_ctx, n_seq, True, refs[count:])
    length = q_ref.shape[0]
    scale = 1.0 / math.sqrt(QK_DIM)

    barrier = pltpu.get_barrier_semaphore()
    for peer in earlier.partner:
        pl.semaphore_signal(barrier, inc=1, device_id=peer, device_id_type=MESH)

    @pl.when(earlier.has_above)
    def _():
        pl.semaphore_signal(barrier, inc=1, device_id=earlier.above, device_id_type=MESH)

    @pl.when(earlier.has_below)
    def _():
        pl.semaphore_signal(barrier, inc=1, device_id=earlier.below, device_id_type=MESH)

    place = earlier.place
    pl.semaphore_wait(
        barrier,
        earlier.rounds + (place + n_ctx - 1) // n_ctx + (n_ctx - 1 - place + n_ctx - 1) // n_ctx,
    )

    gq_acc[...] = jnp.zeros_like(gq_acc)
    gk_acc[...] = jnp.zeros_like(gk_acc)

    def wide(head):
        return pl.ds(pl.multiple_of(head * HEAD_DIM, HEAD_DIM), HEAD_DIM)

    def key_state(head):
        phi = split(features_by_row(a_ref[head], b_ref[head], auxc_ref, k_ref[...]))
        ones = jnp.ones((8, length), jnp.bfloat16)
        put_state(earlier.x, head, dot2(phi, v_ref[:, wide(head)]), dot2r(ones, phi, NT))
        earlier.swap(head).start()

    def middle(head):
        q, k, v, g = q_ref[...], k_ref[...], v_ref[:, wide(head)], g_ref[:, wide(head)]
        pick_a, pick_b = a_ref[head], b_ref[head]
        mine = lax.broadcasted_iota(jnp.int32, (length, LANES), 1) // QK_DIM == head
        q_mine = jnp.where(mine, q, jnp.zeros_like(q))
        k_mine = jnp.where(mine, k, jnp.zeros_like(k))
        s = dot(q_mine, k, NT) * scale
        causal = lax.broadcasted_iota(jnp.int32, (length, length), 0) >= lax.broadcasted_iota(
            jnp.int32, (length, length), 1
        )
        kern = split(jnp.where(causal, 1.0 + s + 0.5 * s * s, 0.0))
        local = dot2(kern, jnp.concatenate([v, jnp.ones_like(v)], axis=1))
        a, b = factors_by_token(pick_a, pick_b, aux_ref, q)
        phi = a * b * aux_ref[2:3, :]
        state = earlier.result(head)
        prior = split(state)
        prior_norm = norm_of(state)
        den = local[:, HEAD_DIM:] + jnp.sum(phi * prior_norm, axis=1, keepdims=True)
        rden = 1.0 / den
        out = (local[:, :HEAD_DIM] + dot3(split(phi), prior)) * rden
        out_ref[:, wide(head)] = out.astype(jnp.bfloat16)
        g32 = g.astype(jnp.float32)
        scaled = split(g32 * rden)
        weighed = g32 * out * rden
        share = jnp.sum(weighed, axis=1, keepdims=True)
        share_row = split(dot2r(jnp.ones((8, LANES), jnp.bfloat16), split(weighed), NT))
        phi_row = split(features_by_row(pick_a, pick_b, auxc_ref, q))
        put_state(later.x, head, dot3(phi_row, scaled), dot3(share_row, phi_row, NT))
        later.swap(head).start()
        rden_column = rden[:, 0:1]
        direct = dot(g, v, NT) * rden_column - share
        grad_dots = split(jnp.where(causal, direct * (1.0 + s) * scale, 0.0))
        gv_acc[:, wide(head)] = dot3(kern, scaled, TN)
        grad_phi = dot2r(g, prior, NT) * rden_column - share * prior_norm
        gq_acc[...] += dot2(grad_dots, k_mine) + pull(
            grad_phi * aux_ref[2:3, :], a, b, pick_a, pick_b
        )
        gk_acc[...] += dot2(grad_dots, q_mine, TN)

    def last(head):
        k, v = k_ref[...], v_ref[:, wide(head)]
        pick_a, pick_b = a_ref[head], b_ref[head]
        state = later.result(head)
        after = split(state)
        a, b = factors_by_token(pick_a, pick_b, aux_ref, k)
        factor = aux_ref[2:3, :]
        grad_v = gv_acc[:, wide(head)] + dot3(split(a * b * factor), after)
        gv_ref[:, wide(head)] = grad_v.astype(jnp.bfloat16)
        grad_phi = dot2r(v, after, NT) - norm_of(state)
        gk_acc[...] += pull(grad_phi * factor, a, b, pick_a, pick_b)

    early_stages, early_done = earlier.stages(0, lags)
    late_stages, late_done = later.stages(early_done, lags)
    plan = list(reversed(late_stages)) + list(reversed(early_stages)) + [
        (key_state, 0, None),
        (middle, early_done, None),
        (last, late_done, None),
    ]

    def turn(t, carry):
        for body, start, condition in plan:
            head = t - start
            ok = (head >= 0) & (head < HEADS)

            @pl.when(ok if condition is None else ok & condition)
            def _(body=body, head=head):
                body(head)

        return carry

    lax.fori_loop(0, late_done + HEADS, turn, 0)
    gq_ref[...] = gq_acc[...].astype(jnp.bfloat16)
    gk_ref[...] = gk_acc[...].astype(jnp.bfloat16)

    def finish(c, carry):
        earlier.finish(c)
        later.finish(c)
        return carry

    lax.fori_loop(0, HEADS, finish, 0)


def per_device(n_ctx, n_seq, queries, keys, values, grad_output):
    length = queries.shape[0]
    rounds = n_seq.bit_length() - 1
    f32, bf16 = jnp.float32, jnp.bfloat16
    full = pltpu.VMEM((HEADS, 2, ROWS // 2, LANES), f32)
    half = pltpu.VMEM((HEADS, ROWS // 2, LANES), f32)
    halves = pltpu.VMEM((rounds - 1, HEADS, ROWS // 2, LANES), f32)
    semaphores = pltpu.SemaphoreType.DMA((rounds + 3, HEADS))
    scan = [full, full, half, halves, halves, half, full, full, full, full, full]
    scan += [semaphores, semaphores]
    narrow = pltpu.VMEM((length, LANES), f32)
    vmem = pl.BlockSpec(memory_space=pltpu.VMEM)
    return pl.pallas_call(
        functools.partial(kernel, n_ctx, n_seq, (1, 2, 1, 2)),
        out_shape=(
            jax.ShapeDtypeStruct(values.shape, bf16),
            jax.ShapeDtypeStruct(queries.shape, bf16),
            jax.ShapeDtypeStruct(keys.shape, bf16),
            jax.ShapeDtypeStruct(values.shape, bf16),
        ),
        in_specs=[vmem] * 8,
        out_specs=(vmem,) * 4,
        scratch_shapes=[narrow, narrow, pltpu.VMEM(values.shape, f32)] + scan + scan,
        compiler_params=pltpu.CompilerParams(
            collective_id=0, has_side_effects=True, vmem_limit_bytes=56 << 20
        ),
        name="attention",
    )(queries, keys, values, grad_output, *tables())


def solution(mesh):
    placed = P(("seq", "ctx"), None)
    return jax.shard_map(
        functools.partial(per_device, mesh.shape["ctx"], mesh.shape["seq"]),
        mesh=mesh,
        in_specs=(placed,) * 4,
        out_specs=(placed,) * 4,
        check_vma=False,
    )
```

time: 404 us -> 72.4 us (0.18)
  waiting for transfers between devices: 178 us -> 0 us
  blocking collectives: 78.5 us -> 0 us
  Pallas kernels: 0 us -> 67.3 us
  other arithmetic: 55.9 us -> 0 us
  local copies, waits for them, and re-layouts: 39.8 us -> 4.22 us
  matrix products: 33.9 us -> 0 us
  between operations: 14.7 us -> 0.66 us
    psum x2 -> x0, waiting for transfers between devices: 96.5 us -> none  [combine(): total = lax.psum((pair[0], pair[1]), 'ctx')]
    all_gather x4 -> x0, waiting for transfers between devices: 79.1 us -> none  [carried_in(): gathered = jax.tree.map(lambda a: lax.all_gather(a, axis), part)]
    pallas_call x0 -> x1, Pallas kernels: none -> 67.3 us  [per_device(): pl.pallas_call(functools.partial(kernel, n_ctx, n_seq, (1, 2, 1, 2)), out...]
    all_gather x4 -> x0, blocking collectives: 57 us -> none  [carried_in(): gathered = jax.tree.map(lambda a: lax.all_gather(a, axis), part)]
    scatter-add x4 -> x0, other arithmetic: 41.7 us -> none  [the longest x2 23.5 us: features(): entries[:, lower, :]]
    dot_general x14 -> x0, matrix products: 33.9 us -> none  [the longest x1 3.73 us: per_device(): jnp.einsum('hfe,the->hft', prior_state, scaled, precision=HIGHEST)]
    psum x2 -> x0, blocking collectives: 21.5 us -> none  [combine(): total = lax.psum((pair[0], pair[1]), 'ctx')]
    dynamic_slice x10 -> x0, local copies, waits for them, and re-layouts: 11.4 us -> none  [one(): lax.dynamic_index_in_dim(a, source, 0, False)]
  transfers between devices with their start and end apart: 6 -> 0, of which waited for: 5 -> 0; matrix products, arithmetic and copies ran while one was open for 8% -> 0% of each run, Pallas kernels for 0% -> 0%
where the time goes in v3:
time: 72.4 us; the launch traced here: 72.2 us
  Pallas kernels  67.3 us (93%)
  local copies, waits for them, and re-layouts  4.22 us (6%)
    pallas_call x1, Pallas kernels, per_device(): pl.pallas_call(functools.partial(kernel, n_ctx, n_seq, (1, 2, 1, 2)), out...  67.3 us
    unnamed x10, local copies, waits for them, and re-layouts  4.22 us

profile of v3, /device:TPU:0, one launch (start us, length us, event | category | flops | bytes accessed | tf_op | source)
XLA Modules:
  0.0 72.2 jit_solution(17902922639334737519)
XLA Ops:
  0.6 67.3 %attention.1 = (bf16[256,1024]{1,0:T(8,128)(2,1)}, bf16[256,128]{1,0:T(8,128)(2,1)}, bf16[256,128]{1,0:T(8,128)(2,1)}, bf16[256,1024]{1,0:T(8,128)(2,1)}) custom-call(bf16[256,128]{1,0:T(8,128)(2,1)} %q_ref.1, bf16[256,128]{1,0:T(8,128)(2,1)} %k_ref.1, bf16[256,1024]{1,0:T(8,128)(2,1)} %v_ref.1, bf16[256,1024]{1,0:T(8,128)(2,1)} %g_ref.1, ...), custom_call_target="tpu_custom_call" | custom-call | tf_op jit(solution)/shard_map/attention/pallas_call | solution.py:369
  68.0 0.0 copy-start.2
  68.0 0.0 copy-start
  68.0 1.9 %copy.16 = bf16[256,1024]{1,0:T(8,128)(2,1)} copy(bf16[256,1024]{1,0:T(8,128)(2,1)} %get-tuple-element.8) | data formatting | bytes 1048576
  69.9 0.0 copy-done.2
  69.9 0.0 copy-start.1
  69.9 0.6 copy.17
  70.5 0.2 copy-done.1
  70.8 0.6 copy.18
  71.4 0.0 copy-done
  71.4 0.8 %copy.19 = bf16[256,1024]{1,0:T(8,128)(2,1)} copy(bf16[256,1024]{1,0:T(8,128)(2,1)S(1)} %copy-done) | data formatting | bytes 1048576
Async XLA Ops:
  68.0 2.0 %copy-start.2 = (bf16[256,128]{1,0:T(8,128)(2,1)S(1)}, bf16[256,128]{1,0:T(8,128)(2,1)}, u32[]{:S(2)}) copy-start(bf16[256,128]{1,0:T(8,128)(2,1)} %get-tuple-element.9) | copy-start | bytes 196612
  68.0 3.4 %copy-start = (bf16[256,1024]{1,0:T(8,128)(2,1)S(1)}, bf16[256,1024]{1,0:T(8,128)(2,1)}, u32[]{:S(2)}) copy-start(bf16[256,1024]{1,0:T(8,128)(2,1)} %get-tuple-element.11) | copy-start | bytes 1572868
  69.9 0.9 %copy-start.1 = (bf16[256,128]{1,0:T(8,128)(2,1)S(1)}, bf16[256,128]{1,0:T(8,128)(2,1)}, u32[]{:S(2)}) copy-start(bf16[256,128]{1,0:T(8,128)(2,1)} %get-tuple-element.10) | copy-start | bytes 196612

commit v4 on v3

--- a/solution.py
+++ b/solution.py
@@ -354,6 +354,15 @@
     lax.fori_loop(0, HEADS, finish, 0)
 
 
+def deliver(*refs):
+    sem = refs[8]
+    copies = [pltpu.make_async_copy(refs[i], refs[4 + i], sem.at[i]) for i in range(4)]
+    for copy in copies:
+        copy.start()
+    for copy in copies:
+        copy.wait()
+
+
 def per_device(n_ctx, n_seq, queries, keys, values, grad_output):
     length = queries.shape[0]
     rounds = n_seq.bit_length() - 1
@@ -366,7 +375,7 @@
     scan += [semaphores, semaphores]
     narrow = pltpu.VMEM((length, LANES), f32)
     vmem = pl.BlockSpec(memory_space=pltpu.VMEM)
-    return pl.pallas_call(
+    results = pl.pallas_call(
         functools.partial(kernel, n_ctx, n_seq, (1, 2, 1, 2)),
         out_shape=(
             jax.ShapeDtypeStruct(values.shape, bf16),
@@ -382,6 +391,16 @@
         ),
         name="attention",
     )(queries, keys, values, grad_output, *tables())
+    anywhere = pl.BlockSpec(memory_space=pl.ANY)
+    inside = pl.BlockSpec(memory_space=pltpu.VMEM)
+    return pl.pallas_call(
+        deliver,
+        out_shape=tuple(jax.ShapeDtypeStruct(a.shape, a.dtype) for a in results),
+        in_specs=[inside] * 4,
+        out_specs=(anywhere,) * 4,
+        scratch_shapes=[pltpu.SemaphoreType.DMA((4,))],
+        name="deliver",
+    )(*results)
 
 
 def solution(mesh):

time: 72.4 us -> 70.4 us (0.972)
  local copies, waits for them, and re-layouts: 4.22 us -> 0 us
  Pallas kernels: 67.3 us -> 69.6 us
    unnamed x10 -> x0, local copies, waits for them, and re-layouts: 4.22 us -> none
    pallas_call x0 -> x1, Pallas kernels: none -> 2.3 us  [per_device(): pl.pallas_call(deliver, out_shape=tuple((jax.ShapeDtypeStruct(a.shape, a....]
where the time goes in v4:
time: 70.4 us; the launch traced here: 70.3 us
  Pallas kernels  69.6 us (99%)
    pallas_call x1, Pallas kernels, per_device(): pl.pallas_call(functools.partial(kernel, n_ctx, n_seq, (1, 2, 1, 2)), out...  67.3 us
    pallas_call x1, Pallas kernels, per_device(): pl.pallas_call(deliver, out_shape=tuple((jax.ShapeDtypeStruct(a.shape, a....  2.3 us

profile of v4, /device:TPU:0, one launch (start us, length us, event | category | flops | bytes accessed | tf_op | source)
XLA Modules:
  0.0 70.3 jit_solution(10343013911224642136)
XLA Ops:
  0.6 67.3 %attention.1 = (bf16[256,1024]{1,0:T(8,128)(2,1)}, bf16[256,128]{1,0:T(8,128)(2,1)}, bf16[256,128]{1,0:T(8,128)(2,1)}, bf16[256,1024]{1,0:T(8,128)(2,1)}) custom-call(bf16[256,128]{1,0:T(8,128)(2,1)} %q_ref.1, bf16[256,128]{1,0:T(8,128)(2,1)} %k_ref.1, bf16[256,1024]{1,0:T(8,128)(2,1)} %v_ref.1, bf16[256,1024]{1,0:T(8,128)(2,1)} %g_ref.1, ...), custom_call_target="tpu_custom_call" | custom-call | tf_op jit(solution)/shard_map/attention/pallas_call | solution.py:378
  68.0 2.3 %deliver.1 = (bf16[256,1024]{1,0:T(8,128)(2,1)}, bf16[256,128]{1,0:T(8,128)(2,1)}, bf16[256,128]{1,0:T(8,128)(2,1)}, bf16[256,1024]{1,0:T(8,128)(2,1)}) custom-call(bf16[256,1024]{1,0:T(8,128)(2,1)} %get-tuple-element.8.refs_0_, bf16[256,128]{1,0:T(8,128)(2,1)} %get-tuple-element.9.refs_1_, bf16[256,128]{1,0:T(8,128)(2,1)} %get-tuple-element.10.refs_2_, ...), custom_call_target="tpu_custom_call" | custom-call | tf_op jit(solution)/shard_map/deliver/pallas_call | solution.py:396

commit v5 on v4

--- a/solution.py
+++ b/solution.py
@@ -234,7 +234,7 @@
 
 def kernel(
     n_ctx, n_seq, lags, q_ref, k_ref, v_ref, g_ref, a_ref, b_ref, aux_ref, auxc_ref,
-    out_ref, gq_ref, gk_ref, gv_ref, gq_acc, gk_acc, gv_acc, *refs,
+    out_ref, gq_ref, gk_ref, gv_ref, gq_acc, gk_acc, gv_acc, rden_kept, share_kept, local_kept, *refs,
 ):
     count = len(refs) // 2
     earlier = Scan(n_ctx, n_seq, False, refs[:count])
@@ -272,18 +272,21 @@
         put_state(earlier.x, head, dot2(phi, v_ref[:, wide(head)]), dot2r(ones, phi, NT))
         earlier.swap(head).start()
 
-    def middle(head):
-        q, k, v, g = q_ref[...], k_ref[...], v_ref[:, wide(head)], g_ref[:, wide(head)]
-        pick_a, pick_b = a_ref[head], b_ref[head]
+    def prepare(head):
+        q, k, v = q_ref[...], k_ref[...], v_ref[:, wide(head)]
         mine = lax.broadcasted_iota(jnp.int32, (length, LANES), 1) // QK_DIM == head
         q_mine = jnp.where(mine, q, jnp.zeros_like(q))
-        k_mine = jnp.where(mine, k, jnp.zeros_like(k))
         s = dot(q_mine, k, NT) * scale
         causal = lax.broadcasted_iota(jnp.int32, (length, length), 0) >= lax.broadcasted_iota(
             jnp.int32, (length, length), 1
         )
         kern = split(jnp.where(causal, 1.0 + s + 0.5 * s * s, 0.0))
-        local = dot2(kern, jnp.concatenate([v, jnp.ones_like(v)], axis=1))
+        local_kept[head] = dot2(kern, jnp.concatenate([v, jnp.ones_like(v)], axis=1))
+
+    def middle(head):
+        q, g = q_ref[...], g_ref[:, wide(head)]
+        pick_a, pick_b = a_ref[head], b_ref[head]
+        local = local_kept[head]
         a, b = factors_by_token(pick_a, pick_b, aux_ref, q)
         phi = a * b * aux_ref[2:3, :]
         state = earlier.result(head)
@@ -301,6 +304,27 @@
         phi_row = split(features_by_row(pick_a, pick_b, auxc_ref, q))
         put_state(later.x, head, dot3(phi_row, scaled), dot3(share_row, phi_row, NT))
         later.swap(head).start()
+        rden_kept[head] = rden
+        share_kept[head] = jnp.broadcast_to(share, rden.shape)
+
+    def local_gradients(head):
+        q, k, v, g = q_ref[...], k_ref[...], v_ref[:, wide(head)], g_ref[:, wide(head)]
+        pick_a, pick_b = a_ref[head], b_ref[head]
+        mine = lax.broadcasted_iota(jnp.int32, (length, LANES), 1) // QK_DIM == head
+        q_mine = jnp.where(mine, q, jnp.zeros_like(q))
+        k_mine = jnp.where(mine, k, jnp.zeros_like(k))
+        s = dot(q_mine, k, NT) * scale
+        causal = lax.broadcasted_iota(jnp.int32, (length, length), 0) >= lax.broadcasted_iota(
+            jnp.int32, (length, length), 1
+        )
+        kern = split(jnp.where(causal, 1.0 + s + 0.5 * s * s, 0.0))
+        a, b = factors_by_token(pick_a, pick_b, aux_ref, q)
+        state = earlier.result(head)
+        prior = split(state)
+        prior_norm = norm_of(state)
+        rden = rden_kept[head]
+        share = share_kept[head][:, 0:1]
+        scaled = split(g.astype(jnp.float32) * rden)
         rden_column = rden[:, 0:1]
         direct = dot(g, v, NT) * rden_column - share
         grad_dots = split(jnp.where(causal, direct * (1.0 + s) * scale, 0.0))
@@ -327,7 +351,9 @@
     late_stages, late_done = later.stages(early_done, lags)
     plan = list(reversed(late_stages)) + list(reversed(early_stages)) + [
         (key_state, 0, None),
+        (prepare, 3, None),
         (middle, early_done, None),
+        (local_gradients, early_done + 8, None),
         (last, late_done, None),
     ]
 
@@ -373,6 +399,7 @@
     semaphores = pltpu.SemaphoreType.DMA((rounds + 3, HEADS))
     scan = [full, full, half, halves, halves, half, full, full, full, full, full]
     scan += [semaphores, semaphores]
+    kept = pltpu.VMEM((HEADS, length, HEAD_DIM), f32)
     narrow = pltpu.VMEM((length, LANES), f32)
     vmem = pl.BlockSpec(memory_space=pltpu.VMEM)
     results = pl.pallas_call(
@@ -385,7 +412,7 @@
         ),
         in_specs=[vmem] * 8,
         out_specs=(vmem,) * 4,
-        scratch_shapes=[narrow, narrow, pltpu.VMEM(values.shape, f32)] + scan + scan,
+        scratch_shapes=[narrow, narrow, pltpu.VMEM(values.shape, f32), kept, kept, pltpu.VMEM((HEADS, length, 2 * HEAD_DIM), f32)] + scan + scan,
         compiler_params=pltpu.CompilerParams(
             collective_id=0, has_side_effects=True, vmem_limit_bytes=56 << 20
         ),

time: 70.4 us -> 69.3 us (0.984)
  Pallas kernels: 69.6 us -> 68.5 us
    pallas_call x1, Pallas kernels: 67.3 us -> 66.2 us  [per_device(): pl.pallas_call(functools.partial(kernel, n_ctx, n_seq, (1, 2, 1, 2)), out...]
where the time goes in v5:
time: 69.3 us; the launch traced here: 69.1 us
  Pallas kernels  68.5 us (99%)
    pallas_call x1, Pallas kernels, per_device(): pl.pallas_call(functools.partial(kernel, n_ctx, n_seq, (1, 2, 1, 2)), out...  66.2 us
    pallas_call x1, Pallas kernels, per_device(): pl.pallas_call(deliver, out_shape=tuple((jax.ShapeDtypeStruct(a.shape, a....  2.3 us

profile of v5, /device:TPU:0, one launch (start us, length us, event | category | flops | bytes accessed | tf_op | source)
XLA Modules:
  0.0 69.1 jit_solution(17543629539533147833)
XLA Ops:
  0.6 66.2 %attention.1 = (bf16[256,1024]{1,0:T(8,128)(2,1)}, bf16[256,128]{1,0:T(8,128)(2,1)}, bf16[256,128]{1,0:T(8,128)(2,1)}, bf16[256,1024]{1,0:T(8,128)(2,1)}) custom-call(bf16[256,128]{1,0:T(8,128)(2,1)} %q_ref.1, bf16[256,128]{1,0:T(8,128)(2,1)} %k_ref.1, bf16[256,1024]{1,0:T(8,128)(2,1)} %v_ref.1, bf16[256,1024]{1,0:T(8,128)(2,1)} %g_ref.1, ...), custom_call_target="tpu_custom_call" | custom-call | tf_op jit(solution)/shard_map/attention/pallas_call | solution.py:405
  66.8 2.3 %deliver.1 = (bf16[256,1024]{1,0:T(8,128)(2,1)}, bf16[256,128]{1,0:T(8,128)(2,1)}, bf16[256,128]{1,0:T(8,128)(2,1)}, bf16[256,1024]{1,0:T(8,128)(2,1)}) custom-call(bf16[256,1024]{1,0:T(8,128)(2,1)} %get-tuple-element.8.refs_0_, bf16[256,128]{1,0:T(8,128)(2,1)} %get-tuple-element.9.refs_1_, bf16[256,128]{1,0:T(8,128)(2,1)} %get-tuple-element.10.refs_2_, ...), custom_call_target="tpu_custom_call" | custom-call | tf_op jit(solution)/shard_map/deliver/pallas_call | solution.py:423
